TPU v7x, 256 devices: a whole 4x4x8 slice. The times are simulated.
256 devices in a mesh: dp: 16 (over z, x_hi), seq: 4 (over y), tensor: 4 (over x_lo, core).
Axes of the slice: x: 4 (x_hi: 2, x_lo: 2; x = x_hi * 2 + x_lo), y: 4, z: 8, core: 2. Of those that a mesh axis runs over, the one named last changes fastest.
Arguments:
- attention_output_rows: bfloat16 [16, 4096, 4096], P('dp', 'seq', 'tensor'), may hold values from -6 to 6
- projection_result_gradient: bfloat16 [16, 4096, 4096], P('dp', 'seq'), may hold values from -6 to 6
- adapter_down_weight: bfloat16 [4096, 128], P('tensor'), may hold values from -0.09375 to 0.09375
- adapter_up_weight: bfloat16 [128, 4096], P(None, 'tensor'), may hold values from -0.09375 to 0.09375
- output_projection_weight: bfloat16 [4096, 4096], P('tensor'), may hold values from -0.09375 to 0.09375
- adam_first_moments: float32 [2, 128, 4096], P(None, 'dp', 'tensor'), may hold values from -24 to 24
- adam_second_moments: float32 [2, 128, 4096], P(None, 'dp', 'tensor'), may hold values from 1 to 40
- rank_side_projection: float32 [16, 128], replicated, may hold values from -0.5 to 0.5
- width_side_projection: bfloat16 [4096, 256], replicated, may hold values from -0.09375 to 0.09375
- bounds: int32 [16, 2, 16], P('dp'), may hold values from 0 to 4096, as said below
- example_owner_slot: int32 [16, 16], P('dp'), may hold values from 0 to 15, each once within a row
Outputs:
- attention_out_gradient: bfloat16 [16, 4096, 4096], P('dp', 'seq', 'tensor')
- features: float32 [16, 16, 8192], P('dp', ('seq', 'tensor'))
Inputs may be any that keep to these rules, and one draw needn't show every extreme that they name: bounds[s, 0, e] is the first token of example e of pack s and bounds[s, 1, e] its end (exclusive): the first start is 0, each end is the next start, the last end is 4096, every example has one token or more. The tokens of one aligned block of 1024 tokens of a pack belong to at most 8 examples, and every pack has a block whose tokens belong to exactly 8. `example_owner_slot`: each row names every slot once.
All inputs are finite; a program needn't handle non-finite values.
Results may differ from a plain program's by a relative error of at most 0.014.
Values may be sent and summed in bfloat16 or wider, within the bound.
A program may use at most 128 MiB of HBM per device.

v0:
```python
import jax
import jax.numpy as jnp
from jax import lax
from jax.sharding import PartitionSpec as P

TOUCH = 8


ADAPTER_SCALE = 4.0
BETA_ONE = 0.9
BETA_TWO = 0.999
EPSILON = 1e-08


def copy_for_each(shard, axis):
    count = lax.axis_size(axis)
    return lax.all_to_all(
        jnp.broadcast_to(shard[None], (count, *shard.shape)), axis, 0, 0, tiled=True
    )


def taken_together(shard, axis):
    return copy_for_each(shard, axis).sum(axis=0)


def together(arrays, axis):
    ends = [0]
    for a in arrays:
        ends.append(ends[-1] + a.size)
    running = taken_together(jnp.concatenate([a.ravel() for a in arrays]), axis)
    return tuple((running[b:e].reshape(a.shape) for a, b, e in zip(arrays, ends, ends[1:])))


def carried_in(shard, axis, join, neutral):
    place = lax.axis_index(axis)
    gathered = jax.tree.map(
        lambda a, kind: lax.all_gather(a.astype(kind), axis), shard, (jnp.bfloat16, jnp.bfloat16)
    )
    state = jax.tree.map(lambda a, e: jnp.zeros_like(a) + jnp.asarray(e, a.dtype), shard, neutral)

    def one(step, state):
        return join(
            state,
            jax.tree.map(
                lambda a, own: lax.dynamic_index_in_dim(a, step, 0, False).astype(own.dtype),
                gathered,
                shard,
            ),
        )

    return lax.fori_loop(0, place, one, state)


def in_blocks(shard, dim, count):
    before, after = (shard.shape[:dim], shard.shape[dim + 1 :])
    return jnp.moveaxis(shard.reshape(*before, count, -1, *after), dim, 0)


def sent_and_summed(shard, axis, dim):
    pieces = in_blocks(shard, dim, lax.axis_size(axis))
    arrived = lax.all_to_all(pieces, axis, split_axis=0, concat_axis=0, tiled=True)
    return arrived.astype(jnp.float32).sum(axis=0)


def contract_trailing(left, right):
    return lax.dot_general(
        left, right, (((1,), (1,)), ((), ())), preferred_element_type=jnp.float32
    )


def normalize(grads, moments):
    first = BETA_ONE * moments[0] + (1.0 - BETA_ONE) * grads
    second = BETA_TWO * moments[1] + (1.0 - BETA_TWO) * grads * grads
    return (first / (jnp.sqrt(second) + EPSILON)).astype(jnp.bfloat16)


def project(normed, rank_side_projection, right_rows):
    inner = jnp.einsum("kmrd,dc->kmrc", normed, right_rows, preferred_element_type=jnp.float32)
    outer = jnp.einsum(
        "qr,kmrc->kmqc", rank_side_projection, inner, precision=lax.Precision.HIGHEST
    )
    return outer.reshape(outer.shape[0], -1)


def pick_slot(block_parts, index):
    return lax.dynamic_index_in_dim(block_parts, index, 0, keepdims=False)


def carry_on(earlier, later):
    return (later[0] + later[1][:, None, None, None] * earlier[0], earlier[1] * later[1])


def per_device(
    attention_output_rows,
    projection_result_gradient,
    adapter_down_weight,
    adapter_up_weight,
    output_projection_weight,
    adam_first_moments,
    adam_second_moments,
    rank_side_projection,
    width_side_projection,
    bounds,
    example_owner_slot,
):
    packs, blk, width_local = attention_output_rows.shape
    width = projection_result_gradient.shape[2]
    adapter_rank_size = adapter_down_weight.shape[1]
    examples = bounds.shape[2]
    seq_index = lax.axis_index("seq")
    tp_index = lax.axis_index("tensor")
    token_count = attention_output_rows.reshape(packs * blk, width_local)
    gradient_complete = projection_result_gradient.reshape(packs * blk, width)
    gradient_columns = lax.dynamic_slice_in_dim(
        gradient_complete, tp_index * width_local, width_local, 1
    )
    reduced_input = jnp.dot(token_count, adapter_down_weight, preferred_element_type=jnp.float32)
    reduced_gradient = contract_trailing(gradient_columns, adapter_up_weight)
    reduced_input, reduced_gradient = together((reduced_input, reduced_gradient), "tensor")
    reduced_input = reduced_input.astype(jnp.bfloat16)
    reduced_gradient = reduced_gradient.astype(jnp.bfloat16)
    attention_out_gradient = contract_trailing(
        gradient_complete, output_projection_weight
    ) + ADAPTER_SCALE * contract_trailing(reduced_gradient, adapter_down_weight)
    attention_out_gradient = attention_out_gradient.astype(jnp.bfloat16).reshape(
        packs, blk, width_local
    )
    positions = seq_index * blk + jnp.arange(blk, dtype=jnp.int32)
    starts = bounds[:, 0, :]
    example_id = (
        jnp.sum((starts[:, None, :] <= positions[None, :, None]).astype(jnp.int32), axis=2) - 1
    )
    first_id = example_id[:, 0]
    last_id = example_id[:, blk - 1]
    slot_range = jnp.arange(TOUCH, dtype=jnp.int32)
    in_slot = ((example_id - first_id[:, None])[:, :, None] == slot_range).astype(jnp.bfloat16)
    masked_grad = (
        reduced_gradient.reshape(packs, blk, 1, adapter_rank_size) * in_slot[..., None]
    ).reshape(packs, blk, TOUCH * adapter_rank_size)
    masked_in = (
        reduced_input.reshape(packs, blk, 1, adapter_rank_size) * in_slot[..., None]
    ).reshape(packs, blk, TOUCH * adapter_rank_size)
    part_a = jnp.einsum(
        "ptk,ptd->pkd", masked_grad, attention_output_rows, preferred_element_type=jnp.float32
    )
    part_b = jnp.einsum(
        "ptk,ptd->pkd",
        masked_in,
        gradient_columns.reshape(packs, blk, width_local),
        preferred_element_type=jnp.float32,
    )
    parts = ADAPTER_SCALE * jnp.stack(
        [
            part_a.reshape(packs, TOUCH, adapter_rank_size, width_local),
            part_b.reshape(packs, TOUCH, adapter_rank_size, width_local),
        ],
        axis=2,
    )
    block_parts = parts.astype(jnp.bfloat16)
    owner_row = example_owner_slot[0]
    slots = owner_row.shape[0]
    slot_ids = jnp.arange(slots, dtype=jnp.int32)
    stacked_moments = jnp.stack([adam_first_moments, adam_second_moments])
    moments = lax.all_gather(stacked_moments.astype(jnp.bfloat16), "dp", axis=2, tiled=True).astype(
        stacked_moments.dtype
    )
    right_rows = lax.dynamic_slice_in_dim(
        width_side_projection, tp_index * width_local, width_local, 0
    )
    example_range = jnp.arange(examples, dtype=jnp.int32)
    ends = bounds[:, 1, :]
    block_low = seq_index * blk
    start_first = jnp.sum(jnp.where(example_range[None, :] == first_id[:, None], starts, 0), axis=1)
    continued = start_first < block_low
    single = first_id == last_id
    keep_flag = (single & continued).astype(jnp.float32)
    last_part = jax.vmap(pick_slot)(block_parts, last_id - first_id).astype(jnp.float32)
    identity = (jnp.zeros_like(last_part), jnp.ones_like(keep_flag))
    carried, unused_flag = carried_in((last_part, keep_flag), "seq", carry_on, identity)
    incoming = jnp.where(continued[:, None, None, None], carried, jnp.zeros_like(carried))
    head_mask = (slot_range == 0).astype(jnp.float32)
    totals = (
        block_parts.astype(jnp.float32) + head_mask[None, :, None, None, None] * incoming[:, None]
    )
    normed = normalize(totals.reshape(packs * TOUCH, 2, adapter_rank_size, width_local), moments)
    partial_features = project(normed, rank_side_projection, right_rows)
    slot_example = first_id[:, None] + slot_range[None, :]
    clipped = jnp.clip(slot_example, 0, examples - 1)
    end_of = jnp.sum(
        jnp.where(clipped[:, :, None] == example_range[None, None, :], ends[:, None, :], 0), axis=2
    )
    finished = (slot_range[None, :] <= (last_id - first_id)[:, None]) & (end_of <= block_low + blk)
    flat_example = jnp.arange(packs, dtype=jnp.int32)[:, None] * examples + clipped
    target = jnp.take(owner_row, flat_example.reshape(-1))
    placing = ((target[None, :] == slot_ids[:, None]) & finished.reshape(-1)[None, :]).astype(
        jnp.float32
    )
    buffer = jnp.dot(placing, partial_features, precision=lax.Precision.HIGHEST)
    features = sent_and_summed(buffer.astype(jnp.bfloat16), ("seq", "tensor"), 0)
    return (attention_out_gradient, features[None])


def solution(mesh):
    return jax.shard_map(
        per_device,
        mesh=mesh,
        in_specs=(
            P("dp", "seq", "tensor"),
            P("dp", "seq", None),
            P("tensor", None),
            P(None, "tensor"),
            P("tensor", None),
            P(None, "dp", "tensor"),
            P(None, "dp", "tensor"),
            P(),
            P(),
            P("dp", None, None),
            P("dp", None),
        ),
        out_specs=(P("dp", "seq", "tensor"), P("dp", ("seq", "tensor"), None)),
        check_vma=False,
    )
```

profile of v0, /device:TPU:1, one launch (start us, length us, event | category | flops | bytes accessed | tf_op | source)
XLA Modules:
  0.0 181.1 jit_solution(11454830477773777389)
XLA Ops:
  7.2 0.0 copy-start
  7.2 1.6 copy-done
  8.8 1.7 convolution_bitcast_fusion.1
  10.4 2.3 %convolution_bitcast_fusion = f32[131072]{0:T(1024)S(1)} fusion(bf16[128,1024]{1,0:T(8,128)(2,1)} %param.16, bf16[1,1024,4096]{2,1,0:T(8,128)(2,1)} %param.14, s32[]{:T(128)S(6)} %select_n.71), kind=kOutput, calls=%fused_computation.3 | convolution fusion | flops 268435456 | bytes 2883588 | tf_op jit(solution)/shard_map/dot_general | solution.py:66
  12.7 0.1 pad_maximum_fusion
  12.8 4.6 %broadcast_in_dim.33 = f32[4,1,262144]{2,1,0:T(1,128)} broadcast(f32[262144]{0:T(1024)S(1)} %pad_maximum_fusion), dimensions={2} | broadcast | bytes 5242880 | tf_op jit(solution)/shard_map/broadcast_in_dim | solution.py:18
  17.4 8.1 %all-to-all-start = ((f32[4,1,262144]{2,1,0:T(1,128)}), f32[4,1,262144]{2,1,0:T(1,128)}, u32[]{:S(2)}, u32[]{:S(2)}) async-start(f32[4,1,262144]{2,1,0:T(1,128)} %broadcast_in_dim.33), calls=%async_computation | async-start | bytes 8388608 | tf_op jit(solution)/shard_map/all_to_all | solution.py:17
  25.6 0.0 all-gather.4.cloned.1.call-start
  25.6 0.0 copy-done.7
  25.6 0.0 copy-done.8
  25.6 0.6 pad_maximum_fusion.1
  26.2 0.0 all-gather.4.cloned.1.call-update
  26.3 0.0 all-gather.6.cloned.1.call-start
  26.4 0.0 copy-done.10
  26.4 0.1 convert_reduce_fusion.1
  26.5 0.6 fusion.50
  27.1 1.3 fusion.47
  31.6 0.5 fusion.48
  32.1 0.0 copy-done.11
  32.1 0.6 dynamic-slice.5
  32.7 1.4 dynamic-update-slice.1
  34.1 0.6 fusion.49
  34.7 0.6 broadcast_subtract_fusion
  35.4 38.2 %all-to-all-done = f32[4,1,262144]{2,1,0:T(1,128)} async-done(((f32[4,1,262144]{2,1,0:T(1,128)}), f32[4,1,262144]{2,1,0:T(1,128)}, u32[]{:S(2)}, u32[]{:S(2)}) %all-to-all-start) | async-done | bytes 4194336 | tf_op jit(solution)/shard_map/all_to_all | solution.py:17
  73.6 9.9 %reduce_sum.45 = bf16[262144]{0:T(1024)(128)(2,1)S(1)} reduce(f32[4,1,262144]{2,1,0:T(1,128)} %all-to-all-done, f32[]{:T(128)} %constant.38.clone.1), dimensions={0,1}, to_apply=%region_0.0 | reduce | flops 786432 | bytes 4718596 | tf_op jit(solution)/shard_map/reduce_sum | solution.py:23
  83.4 0.0 copy-start.4
  83.5 0.1 copy.29
  83.6 0.1 copy.28
  83.8 3.9 %fusion.11 = f32[8,128,1024]{2,1,0:T(8,128)S(1)} fusion(bf16[1,1024,4096]{2,1,0:T(8,128)(2,1)} %param.14, s32[]{:T(128)S(6)} %select_n.71, bf16[1024,128]{0,1:T(8,128)(2,1)S(1)} %copy.29, bf16[1024,8]{0,1:T(8,128)(2,1)S(1)} %fusion.36), kind=kOutput, calls=%fused_computation.22 | convolution fusion | flops 2148532224 | bytes 6569988 | tf_op jit(solution)/shard_map/ptk,ptd->pkd/dot_general | solution.py:146
  87.7 0.0 copy-done.4
  87.7 0.0 copy-start.2
  87.7 2.3 %fusion.13 = f32[8,128,1024]{2,1,0:T(8,128)S(1)} fusion(bf16[1,1024,1024]{2,1,0:T(8,128)(2,1)S(1)} %copy-done, bf16[1024,8]{0,1:T(8,128)(2,1)S(1)} %fusion.36, bf16[1024,128]{0,1:T(8,128)(2,1)S(1)} %copy.28), kind=kOutput, calls=%fused_computation.24 | convolution fusion | flops 2148532224 | bytes 6569984 | tf_op jit(solution)/shard_map/ptk,ptd->pkd/dot_general | solution.py:143
  90.1 0.0 copy-start.3
  90.1 0.0 copy-done.2
  90.1 2.0 %copy-done.3 = f32[8,128,1024]{2,1,0:T(8,128)} copy-done((f32[8,128,1024]{2,1,0:T(8,128)}, f32[8,128,1024]{2,1,0:T(8,128)S(1)}, u32[]{:S(2)}) %copy-start.3) | copy-done | bytes 4194328
  92.0 0.9 fusion.35
  92.9 0.0 all-gather.6.cloned.1.call-update
  93.0 7.2 %all-reduce = bf16[4]{0:T(256)(128)(2,1)S(1)} all-reduce(bf16[4]{0:T(256)(128)(2,1)S(1)} %dynamic-update-slice.1), channel_id=2, replica_groups=mesh['dp'=16,'seq'=4,'tensor'=4] {'seq'}, use_global_device_ids=true, to_apply=%add | all-reduce | flops 4 | bytes 16
  100.1 0.6 gather_fusion
  100.8 0.6 and_select_fusion
  101.4 0.2 select_reduce_fusion
  101.6 15.2 %fusion.6 = f32[1024,1024]{1,0:T(8,128)} fusion(bf16[1024,4096]{1,0:T(8,128)(2,1)} %param.17, bf16[1,1024,4096]{2,1,0:T(8,128)(2,1)} %param.14), kind=kOutput, calls=%fused_computation.16 | convolution fusion | flops 8589934592 | bytes 20971520 | tf_op jit(solution)/shard_map/dot_general | solution.py:66
  116.8 1.5 convert_element_type.102
  118.3 1.6 fusion.28
  119.8 21.2 %all-gather.6.cloned.1.call-done = bf16[4,1,2,128,1024]{4,3,2,1,0:T(8,128)(2,1)} async-done(((bf16[1,1,2,128,1024]{4,3,2,1,0:T(8,128)(2,1)}), bf16[4,1,2,128,1024]{4,3,2,1,0:T(8,128)(2,1)}) %all-gather.6.cloned.1.call-update) | async-done | bytes 2097168 | tf_op jit(solution)/shard_map/all_gather | solution.py:37
  141.0 0.1 broadcast.337
  141.1 0.2 while.13
  141.3 0.1 select_bitcast_fusion
  141.4 0.0 copy-start.9
  141.4 8.1 %fusion.9 = f32[8,2,128,256]{3,2,1,0:T(8,128)S(1)} fusion(bf16[4096,256]{1,0:T(8,128)(2,1)} %param.21, s32[]{:T(128)S(6)} %select_n.71, f32[8,1,128,1024]{3,2,0,1:T(8,128)} %bitcast.113, f32[8,1,128,1024]{3,2,0,1:T(8,128)} %bitcast.115, f32[2,128,1024]{2,1,0:T(8,128)} %get-tuple-element.79, f32[2,128,1024]{2,1,0:T(8,128)S(1)} %select_bitcast_fusion, ...), kind=kOutput, calls=%fused_computation.19 | convolution fusion | flops 1103101952 | bytes 14155812 | tf_op jit(solution)/shard_map/kmrd,dc->kmrc/dot_general | solution.py:78
  149.5 0.0 copy-done.9
  149.5 0.0 copy-start.5
  149.5 0.0 copy-start.6
  149.6 1.2 fusion.37
  150.8 0.2 copy.36
  150.9 0.4 fusion
  151.3 0.5 broadcast.368
  151.8 0.8 reduce.5
  152.6 0.9 reshape.513
  153.5 12.1 %all-to-all-start.1 = ((bf16[16,2,4096]{2,1,0:T(2,128)(2,1)}), bf16[16,2,4096]{2,1,0:T(2,128)(2,1)S(1)}, u32[]{:S(2)}, u32[]{:S(2)}) async-start(bf16[16,2,4096]{2,1,0:T(2,128)(2,1)} %reshape.513), calls=%async_computation.1 | async-start | bytes 524288 | tf_op jit(solution)/shard_map/all_to_all | solution.py:61
  165.6 4.2 %fusion.23 = bf16[1,1024,1024]{2,1,0:T(8,128)(2,1)} fusion(f32[1024,1024]{1,0:T(8,128)} %fusion.6, bf16[1024,128]{1,0:T(8,128)(2,1)S(1)} %copy-done.6, bf16[262144]{0:T(1024)(128)(2,1)S(1)} %copy-done.5), kind=kOutput, calls=%fused_computation.34 | convolution fusion | flops 271581184 | bytes 6815744 | tf_op jit(solution)/shard_map/dot_general | solution.py:66
  169.8 3.0 %all-to-all-done.1 = bf16[16,2,4096]{2,1,0:T(2,128)(2,1)S(1)} async-done(((bf16[16,2,4096]{2,1,0:T(2,128)(2,1)}), bf16[16,2,4096]{2,1,0:T(2,128)(2,1)S(1)}, u32[]{:S(2)}, u32[]{:S(2)}) %all-to-all-start.1) | async-done | bytes 262176 | tf_op jit(solution)/shard_map/all_to_all | solution.py:61
  172.8 0.3 reshape.514
  173.1 1.2 convert_reduce_fusion
  (19 shorter events, 0.1 us)
Async XLA Ops:
  7.2 1.6 copy-start
  17.4 8.2 %copy-start.7 = (f32[2,8,1024]{2,1,0:T(8,128)S(1)}, f32[2,8,1024]{2,1,0:T(8,128)}, u32[]{:S(2)}) copy-start(f32[2,8,1024]{2,1,0:T(8,128)} %param.19) | copy-start | bytes 196612
  17.4 8.2 %copy-start.8 = (f32[2,8,1024]{2,1,0:T(8,128)S(1)}, f32[2,8,1024]{2,1,0:T(8,128)}, u32[]{:S(2)}) copy-start(f32[2,8,1024]{2,1,0:T(8,128)} %param.18) | copy-start | bytes 196612
  17.4 8.9 %copy-start.10 = (s32[1,2,16]{2,1,0:T(2,128)S(1)}, s32[1,2,16]{2,1,0:T(2,128)}, u32[]{:S(2)}) copy-start(s32[1,2,16]{2,1,0:T(2,128)} %param.22) | copy-start | bytes 388
  17.4 14.7 %copy-start.11 = (u32[256]{0:T(256)S(1)}, u32[256]{0:T(256)}, u32[]{:S(2)}) copy-start(u32[256]{0:T(256)} %constant.106) | copy-start | bytes 3076
  17.4 56.1 %all-to-all-start = ((f32[4,1,262144]{2,1,0:T(1,128)}), f32[4,1,262144]{2,1,0:T(1,128)}, u32[]{:S(2)}, u32[]{:S(2)}) async-start(f32[4,1,262144]{2,1,0:T(1,128)} %broadcast_in_dim.33), calls=%async_computation | async-start | bytes 8388608 | tf_op jit(solution)/shard_map/all_to_all | solution.py:17
  25.6 91.2 %all-gather.4.cloned.1.call-start = ((), (), s32[]{:S(2)}) async-start(), calls=%async_computation.2 | async-start | bytes 1114112 | tf_op jit(solution)/shard_map/all_gather | solution.py:164
  26.3 114.7 %all-gather.6.cloned.1.call-start = ((), (), s32[]{:S(2)}) async-start(), calls=%async_computation.3 | async-start | bytes 2621440 | tf_op jit(solution)/shard_map/all_gather | solution.py:37
  83.4 4.3 %copy-start.4 = (bf16[262144]{0:T(1024)(128)(2,1)}, bf16[262144]{0:T(1024)(128)(2,1)S(1)}, u32[]{:S(2)}) copy-start(bf16[262144]{0:T(1024)(128)(2,1)S(1)} %reduce_sum.45) | copy-start | bytes 1572868
  87.7 2.4 %copy-start.2 = (f32[8,128,1024]{2,1,0:T(8,128)}, f32[8,128,1024]{2,1,0:T(8,128)S(1)}, u32[]{:S(2)}) copy-start(f32[8,128,1024]{2,1,0:T(8,128)S(1)} %fusion.11) | copy-start | bytes 12582916
  90.1 2.0 %copy-start.3 = (f32[8,128,1024]{2,1,0:T(8,128)}, f32[8,128,1024]{2,1,0:T(8,128)S(1)}, u32[]{:S(2)}) copy-start(f32[8,128,1024]{2,1,0:T(8,128)S(1)} %fusion.13) | copy-start | bytes 12582916
  92.0 8.1 %copy-start.1 = (s32[1,16]{1,0:T(1,128)S(1)}, s32[1,16]{1,0:T(1,128)}, u32[]{:S(2)}) copy-start(s32[1,16]{1,0:T(1,128)} %param.23) | copy-start | bytes 196
  141.4 8.1 %copy-start.9 = (f32[16,128]{1,0:T(8,128)S(1)}, f32[16,128]{1,0:T(8,128)}, u32[]{:S(2)}) copy-start(f32[16,128]{1,0:T(8,128)} %param.20) | copy-start | bytes 24580
  149.5 16.1 %copy-start.5 = (bf16[262144]{0:T(1024)(128)(2,1)S(1)}, bf16[262144]{0:T(1024)(128)(2,1)}, u32[]{:S(2)}) copy-start(bf16[262144]{0:T(1024)(128)(2,1)} %copy-done.4) | copy-start | bytes 1572868
  149.5 16.1 %copy-start.6 = (bf16[1024,128]{1,0:T(8,128)(2,1)S(1)}, bf16[1024,128]{1,0:T(8,128)(2,1)}, u32[]{:S(2)}) copy-start(bf16[1024,128]{1,0:T(8,128)(2,1)} %param.15) | copy-start | bytes 786436
  153.5 19.3 %all-to-all-start.1 = ((bf16[16,2,4096]{2,1,0:T(2,128)(2,1)}), bf16[16,2,4096]{2,1,0:T(2,128)(2,1)S(1)}, u32[]{:S(2)}, u32[]{:S(2)}) async-start(bf16[16,2,4096]{2,1,0:T(2,128)(2,1)} %reshape.513), calls=%async_computation.1 | async-start | bytes 524288 | tf_op jit(solution)/shard_map/all_to_all | solution.py:61
Sparse Core Ops, SparseCore 0:
  29.5 75.4 all-gather.3
  106.8 34.0 all-gather.5
where the time goes:
time: 182 us; the launch traced here: 181 us
  waiting for transfers between devices  62.4 us (34%)
  matrix products  39.3 us (22%)
  other arithmetic  20.6 us (11%)
  starting transfers between devices  20.3 us (11%)
  between operations  17.5 us (10%)
  local copies, waits for them, and re-layouts  13.7 us (8%)
  blocking collectives  7.17 us (4%)
    all_to_all x1, waiting for transfers between devices, copy_for_each(): lax.all_to_all(jnp.broadcast_to(shard[None], (count, *shard.shape)), axis...  38.2 us
    dot_general x3, matrix products, contract_trailing(): lax.dot_general(left, right, (((1,), (1,)), ((), ())), preferred_element_...  21.7 us
    all_gather x1, waiting for transfers between devices, carried_in(): lax.all_gather(a.astype(kind), axis)  21.2 us
    all_to_all x1, starting transfers between devices, sent_and_summed(): lax.all_to_all(pieces, axis, split_axis=0, concat_axis=0, tiled=True)  12.1 us
    reduce_sum x1, other arithmetic, taken_together(): return copy_for_each(shard, axis).sum(axis=0)  9.85 us
    all_to_all x1, starting transfers between devices, copy_for_each(): lax.all_to_all(jnp.broadcast_to(shard[None], (count, *shard.shape)), axis...  8.14 us
    dot_general x1, matrix products, project(): jnp.einsum('kmrd,dc->kmrc', normed, right_rows, preferred_element_type=jn...  8.12 us
    unnamed x1, blocking collectives  7.17 us
  transfers between devices with their start and end apart: 4, of which 3 were waited for; matrix products, arithmetic and copies ran while one was open for 26% of the time, Pallas kernels for 0%

commit v1 on v0

v1 whole, which is shorter than its diff:
```python
import functools

import jax
import jax.numpy as jnp
from jax import lax
from jax.experimental import pallas as pl
from jax.experimental.pallas import tpu as pltpu
from jax.sharding import PartitionSpec as P

TOUCH = 8
SCALE = 4.0
BETA_ONE = 0.9
BETA_TWO = 0.999
EPSILON = 1e-08

N_DP, N_SEQ, N_TP = 16, 4, 4
GROUP = N_SEQ * N_TP
BLK = 1024
WIDTH = 4096
COLS = WIDTH // N_TP
RANK = 128
KR, KD = 16, 256
EX = 16
HALF = BLK // 2
TILE = 256
CHUNKS = 4
N_Z = 8

bf16 = jnp.bfloat16
f32 = jnp.float32
NT = (((1,), (1,)), ((), ()))
MESH_ID = pl.DeviceIdType.MESH


def kernel(
    x_hbm, g_hbm, a_hbm, b_hbm, w_hbm, m1_hbm, m2_hbm, r_ref, q_hbm, bounds, owner,
    out_hbm, feat_ref,
    xv, gv, wv, av, bv, qv, m1v, m2v, acc, outv,
    ex1s, ex1r, lowh, ex2s, ex2r, low, low_t, lhs, parts, cs, cr, mom, uv, fv, fsend, frecv,
    ld_sem, out_sem, ex_ss, ex_rs, mx_s, mx_r, mz_s, mz_r, c_ss, c_rs, f_ss, f_rs,
):
    dp = lax.axis_index("dp")
    s = lax.axis_index("seq")
    t = lax.axis_index("tensor")
    core = lax.rem(t, 2)
    chip = lax.div(t, 2)
    partner = chip * 2 + (1 - core)
    across = (1 - chip) * 2 + core
    zi = lax.div(dp, 2)
    xh = lax.rem(dp, 2)
    xpeer = zi * 2 + (1 - xh)
    zright = lax.rem(zi + 1, N_Z)
    zleft = lax.rem(zi + N_Z - 1, N_Z)
    me = s * N_TP + t

    barrier = pltpu.get_barrier_semaphore()

    def greet(j, _):
        o = lax.rem(me + j, GROUP)
        pl.semaphore_signal(
            barrier, inc=1, device_id={"seq": lax.div(o, N_TP), "tensor": lax.rem(o, N_TP)},
            device_id_type=MESH_ID)
        return 0

    lax.fori_loop(1, GROUP, greet, 0)
    for peer in (xpeer, zright * 2 + xh, zleft * 2 + xh):
        pl.semaphore_signal(barrier, inc=1, device_id={"dp": peer}, device_id_type=MESH_ID)

    def col(i):
        return pl.ds(pl.multiple_of(lax.rem(t + i, N_TP) * COLS, COLS), COLS)

    def load(i, src, dst):
        return pltpu.make_async_copy(src, dst, ld_sem.at[i])

    ld_a = load(0, a_hbm, av)
    ld_b = load(1, b_hbm, bv)
    ld_x = load(2, x_hbm, xv)
    ld_g = [load(3 + i, g_hbm.at[:, col(i)], gv.at[:, col(i)]) for i in range(N_TP)]
    ld_m1 = load(7, m1_hbm, m1v)
    ld_m2 = load(8, m2_hbm, m2v)
    ld_q = load(9, q_hbm.at[col(0), :], qv)
    ld_w = [
        load(10 + i, w_hbm.at[pl.ds(i * TILE, TILE), :], wv.at[pl.ds(i * TILE, TILE), :])
        for i in range(4)
    ]
    for c in (ld_a, ld_b, ld_x, ld_g[0], ld_m1, ld_m2, *ld_g[1:], *ld_w, ld_q):
        c.start()

    ld_a.wait()
    ld_b.wait()
    ld_x.wait()
    ld_g[0].wait()

    def partial(h):
        rows = pl.ds(pl.multiple_of(h * HALF, HALF), HALF)
        p_in = jnp.dot(xv[rows, :], av[...], preferred_element_type=f32)
        p_gr = lax.dot_general(gv[rows, col(0)], bv[...], NT, preferred_element_type=f32)
        return p_gr, p_in

    p_gr, p_in = partial(1 - core)
    ex1s[:, :RANK] = p_gr.astype(bf16)
    ex1s[:, RANK:] = p_in.astype(bf16)

    pl.semaphore_wait(barrier, GROUP - 1 + 3)

    def rcopy(src, dst, ss, rs, **where):
        return pltpu.make_async_remote_copy(
            src_ref=src, dst_ref=dst, send_sem=ss, recv_sem=rs, device_id=where,
            device_id_type=MESH_ID)

    ex1 = rcopy(ex1s, ex1r, ex_ss.at[0], ex_rs.at[0], tensor=partner)
    ex1.start()

    ld_m1.wait()
    ld_m2.wait()
    for m in range(2):
        mom[zi, xh, m] = jnp.concatenate([m1v[m], m2v[m]], axis=0).astype(bf16)
    mx = rcopy(mom.at[zi, xh], mom.at[zi, xh], mx_s, mx_r, dp=xpeer)
    mx.start()
    mx_in = rcopy(mom.at[zi, xh], mom.at[zi, 1 - xh], mx_s, mx_r, dp=xpeer)

    p_gr, p_in = partial(core)
    lowh[:, :RANK] = p_gr
    lowh[:, RANK:] = p_in

    right_dp = zright * 2 + xh
    left_dp = zleft * 2 + xh

    def ring(j):
        zr = lax.rem(zi + N_Z - j, N_Z)
        zl = lax.rem(zi + j, N_Z)
        if j < 3:
            a = mom.at[zr]
            b = mom.at[zl]
        else:
            a = mom.at[zr, 0]
            b = mom.at[zl, 1]
        return (
            rcopy(a, a, mz_s.at[j, 0], mz_r.at[j, 0], dp=right_dp),
            rcopy(b, b, mz_s.at[j, 1], mz_r.at[j, 1], dp=left_dp),
        )

    def ring_in(j):
        zr = lax.rem(zi + N_Z - j - 1, N_Z)
        zl = lax.rem(zi + j + 1, N_Z)
        if j < 3:
            a = mom.at[zr]
            b = mom.at[zl]
        else:
            a = mom.at[zr, 0]
            b = mom.at[zl, 1]
        return (
            rcopy(a, a, mz_s.at[j, 0], mz_r.at[j, 0], dp=right_dp),
            rcopy(b, b, mz_s.at[j, 1], mz_r.at[j, 1], dp=left_dp),
        )

    def ring_start(j):
        for c in ring(j):
            c.start()

    def ring_wait(j):
        for c in ring_in(j):
            c.wait_recv()

    def main_tile(n):
        acc[:, n * TILE:(n + 1) * TILE] = lax.dot_general(
            gv[...], wv[n * TILE:(n + 1) * TILE, :], NT, preferred_element_type=f32)

    for c in ld_g[1:]:
        c.wait()
    ld_w[0].wait()
    main_tile(0)

    ex1.wait_recv()
    total = lowh[...] + ex1r[...].astype(f32)
    lowh[...] = total
    ex2s[...] = total.astype(bf16)
    ex2 = rcopy(ex2s, ex2r, ex_ss.at[1], ex_rs.at[1], tensor=across)
    ex2.start()

    mx_in.wait_recv()
    ring_start(0)
    ld_w[1].wait()
    main_tile(1)
    ld_w[2].wait()
    main_tile(2)
    ring_wait(0)
    ring_start(1)
    ld_w[3].wait()
    main_tile(3)

    ex2.wait_recv()
    low[core] = (lowh[...] + ex2r[...].astype(f32)).astype(bf16)
    ex3 = rcopy(low.at[core], low.at[core], ex_ss.at[2], ex_rs.at[2], tensor=partner)
    ex3_in = rcopy(low.at[1 - core], low.at[1 - core], ex_ss.at[2], ex_rs.at[2], tensor=partner)
    ex3.start()

    low_pos = s * BLK
    n_le = jnp.int32(0)
    n_lt = jnp.int32(0)
    n_last = jnp.int32(0)
    pos = low_pos + lax.broadcasted_iota(jnp.int32, (1, BLK), 1)
    slot = jnp.zeros((1, BLK), jnp.int32)
    for e in range(EX):
        st = bounds[0, e]
        n_le = n_le + (st <= low_pos).astype(jnp.int32)
        n_lt = n_lt + (st < low_pos).astype(jnp.int32)
        n_last = n_last + (st <= low_pos + BLK - 1).astype(jnp.int32)
        slot = slot + (st <= pos).astype(jnp.int32)
    first_id = n_le - 1
    last_id = n_last - 1
    slot = slot - n_le
    n_slots = last_id - first_id
    continued = (n_le == n_lt).astype(f32)
    keep = continued * (first_id == last_id).astype(f32)

    ex3_in.wait_recv()
    for h in range(2):
        low_t[:, h * HALF:(h + 1) * HALF] = (low[h].astype(f32) * SCALE).T.astype(bf16)

    m_last = (slot == n_slots).astype(f32).astype(bf16)
    for m in range(2):
        left = low_t[m * RANK:(m + 1) * RANK, :] * m_last
        right = xv[...] if m == 0 else gv[:, col(0)]
        p = jnp.dot(left, right, preferred_element_type=f32).astype(bf16)
        cs[2 * m] = p[:64]
        cs[2 * m + 1] = p[64:]

    @pl.when(s == 0)
    def _():
        cr[...] = jnp.zeros_like(cr)

    nxt = lax.rem(s + 1, N_SEQ)

    def chain_copy(c):
        return rcopy(cs.at[c], cr.at[c], c_ss.at[c], c_rs.at[c], seq=nxt)

    def chain(p):
        c = p - s

        @pl.when((c >= 0) & (c < CHUNKS) & (s < N_SEQ - 1))
        def _():
            @pl.when(s > 0)
            def _():
                chain_copy(c).wait_recv()
                cs[c] = (cs[c].astype(f32) + keep * cr[c].astype(f32)).astype(bf16)

            chain_copy(c).start()

    chain(0)

    def build(m):
        def one(k, _):
            mask = (slot == k).astype(f32).astype(bf16)
            lhs[pl.ds(pl.multiple_of(k * RANK, RANK), RANK), :] = (
                low_t[m * RANK:(m + 1) * RANK, :] * mask)
            return 0

        lax.fori_loop(0, TOUCH, one, 0)

    def part_tiles(m):
        def one(n, _):
            c0 = pl.ds(pl.multiple_of(n * TILE, TILE), TILE)
            if m == 0:
                right = xv[:, c0]
            else:
                right = gv[:, pl.ds(pl.multiple_of(t * COLS + n * TILE, TILE), TILE)]
            parts[m, :, c0] = jnp.dot(lhs[...], right, preferred_element_type=f32).astype(bf16)
            return 0

        lax.fori_loop(0, COLS // TILE, one, 0)

    ring_wait(1)
    ring_start(2)
    build(0)
    part_tiles(0)
    chain(1)
    build(1)
    part_tiles(1)
    chain(2)
    ring_wait(2)
    ring_start(3)

    def fix(i, _):
        rows = pl.ds(pl.multiple_of(i * TILE, TILE), TILE)
        h = lax.div(i, 2)
        sub = pl.ds(pl.multiple_of(lax.rem(i, 2) * TILE, TILE), TILE)
        lg = low[h, sub, :RANK]
        corr = lax.dot_general(lg, av[...], NT, preferred_element_type=f32)
        outv[rows, :] = (acc[rows, :] + SCALE * corr).astype(bf16)
        return 0

    lax.fori_loop(0, BLK // TILE, fix, 0)
    out_copy = pltpu.make_async_copy(outv, out_hbm, out_sem)
    out_copy.start()
    chain(3)

    r = r_ref[...]
    r_hi = r.astype(bf16)
    r_lo = (r - r_hi.astype(f32)).astype(bf16)
    r2 = jnp.concatenate([r_hi, r_lo], axis=0)

    def normalized(k, m, incoming):
        for c in range(COLS // TILE):
            cc = slice(c * TILE, (c + 1) * TILE)
            rows = []
            for d in range(0, N_DP, 2):
                a = mom[d // 2, 0, m, :, cc].astype(f32)
                b = mom[d // 2, 1, m, :, cc].astype(f32)
                m1 = jnp.concatenate([a[:8], b[:8]], axis=0)
                m2 = jnp.concatenate([a[8:], b[8:]], axis=0)
                g = parts[m, pl.ds(pl.multiple_of(k * RANK + d * 8, 16), 16), cc].astype(f32)
                if incoming:
                    ch = 2 * m + d // 8
                    g = g + continued * cr[ch, (d % 8) * 8:(d % 8) * 8 + 16, cc].astype(f32)
                first = BETA_ONE * m1 + (1.0 - BETA_ONE) * g
                second = BETA_TWO * m2 + (1.0 - BETA_TWO) * (g * g)
                root = second * lax.rsqrt(second) + EPSILON
                rows.append((first * lax.rsqrt(root * root)).astype(bf16))
            n = jnp.concatenate(rows, axis=0)
            u = jnp.dot(r2, n, preferred_element_type=f32)
            u = u[:KR] + u[KR:]
            hi = u.astype(bf16)
            uv[k, m, 0, :, cc] = hi
            uv[k, m, 1, :, cc] = (u - hi.astype(f32)).astype(bf16)

    def slots(lo, hi):
        def one(i, _):
            normalized(lax.div(i, 2), lax.rem(i, 2), False)
            return 0

        lax.fori_loop(2 * lo, 2 * hi, one, 0)

    ring_wait(3)
    ld_q.wait()
    slots(1, 3)
    chain(4)
    slots(3, 6)
    chain(5)
    slots(6, 8)

    @pl.when(s == N_SEQ - 1)
    def _():
        for c in range(CHUNKS):
            chain_copy(c).wait_recv()

    for m in range(2):
        normalized(0, m, True)

    def widths(k, _):
        u = uv[k].reshape(2 * 2 * KR, COLS)
        f = jnp.dot(u, qv[...], preferred_element_type=f32)
        fv[k, :KR] = f[:KR] + f[KR:2 * KR]
        fv[k, KR:] = f[2 * KR:3 * KR] + f[3 * KR:]
        return 0

    lax.fori_loop(0, TOUCH, widths, 0)

    goes = []
    for k in range(TOUCH):
        e = jnp.minimum(first_id + k, EX - 1)
        done = (k <= n_slots) & (bounds[1, e] <= low_pos + BLK)
        goes.append(jnp.where(done, owner[0, e], -1))

    def place(o, _):
        total = jnp.zeros((2 * KR, KD), f32)
        for k in range(TOUCH):
            total = total + jnp.where(goes[k] == o, 1.0, 0.0) * fv[k]
        fsend[o] = total.astype(bf16)
        return 0

    lax.fori_loop(0, GROUP, place, 0)

    def feature_copy(o, j):
        return rcopy(
            fsend.at[o], frecv.at[me], f_ss.at[j], f_rs.at[me],
            seq=lax.div(o, N_TP), tensor=lax.rem(o, N_TP))

    def send_out(j, _):
        feature_copy(lax.rem(me + j, GROUP), j).start()
        return 0

    lax.fori_loop(1, GROUP, send_out, 0)
    frecv[me] = fsend[me]

    def arrive(j, _):
        o = lax.rem(me + j, GROUP)
        rcopy(fsend.at[o], frecv.at[o], f_ss.at[j], f_rs.at[o],
              seq=lax.div(o, N_TP), tensor=lax.rem(o, N_TP)).wait_recv()
        return 0

    lax.fori_loop(1, GROUP, arrive, 0)
    feat = jnp.zeros((2 * KR, KD), f32)
    for o in range(GROUP):
        feat = feat + frecv[o].astype(f32)
    feat_ref[...] = feat

    ex1.wait_send()
    ex2.wait_send()
    ex3.wait_send()
    mx.wait_send()
    for j in range(4):
        for c in ring(j):
            c.wait_send()

    @pl.when(s < N_SEQ - 1)
    def _():
        for c in range(CHUNKS):
            chain_copy(c).wait_send()

    def left(j, _):
        feature_copy(lax.rem(me + j, GROUP), j).wait_send()
        return 0

    lax.fori_loop(1, GROUP, left, 0)
    out_copy.wait()


def per_device(x, g, a, b, w, m1, m2, r, q, bounds, owner):
    any_ = pl.BlockSpec(memory_space=pl.ANY)
    vmem = pl.BlockSpec(memory_space=pltpu.VMEM)
    smem = pl.BlockSpec(memory_space=pltpu.SMEM)
    dma = pltpu.SemaphoreType.DMA
    V = pltpu.VMEM
    att, feat = pl.pallas_call(
        kernel,
        out_shape=(
            jax.ShapeDtypeStruct((BLK, COLS), bf16),
            jax.ShapeDtypeStruct((2 * KR, KD), f32),
        ),
        in_specs=[any_] * 7 + [vmem, any_, smem, smem],
        out_specs=(any_, vmem),
        scratch_shapes=[
            V((BLK, COLS), bf16), V((BLK, WIDTH), bf16), V((COLS, WIDTH), bf16),
            V((COLS, RANK), bf16), V((RANK, COLS), bf16), V((COLS, KD), bf16),
            V((2, 8, COLS), f32), V((2, 8, COLS), f32),
            V((BLK, COLS), f32), V((BLK, COLS), bf16),
            V((HALF, 2 * RANK), bf16), V((HALF, 2 * RANK), bf16), V((HALF, 2 * RANK), f32),
            V((HALF, 2 * RANK), bf16), V((HALF, 2 * RANK), bf16),
            V((2, HALF, 2 * RANK), bf16), V((2 * RANK, BLK), bf16),
            V((TOUCH * RANK, BLK), bf16), V((2, TOUCH * RANK, COLS), bf16),
            V((CHUNKS, 64, COLS), bf16), V((CHUNKS, 64, COLS), bf16),
            V((N_Z, 2, 2, 16, COLS), bf16),
            V((TOUCH, 2, 2, KR, COLS), bf16), V((TOUCH, 2 * KR, KD), f32),
            V((GROUP, 2 * KR, KD), bf16), V((GROUP, 2 * KR, KD), bf16),
            dma((14,)), dma(()), dma((3,)), dma((3,)), dma(()), dma(()),
            dma((4, 2)), dma((4, 2)), dma((CHUNKS,)), dma((CHUNKS,)),
            dma((GROUP,)), dma((GROUP,)),
        ],
        compiler_params=pltpu.CompilerParams(
            collective_id=0, has_side_effects=True, vmem_limit_bytes=60 * 2**20),
        name="step",
    )(
        x.reshape(BLK, COLS), g.reshape(BLK, WIDTH), a, b, w, m1, m2, r, q,
        bounds.reshape(2, EX), owner.reshape(1, EX),
    )
    return att.reshape(1, BLK, COLS), feat.reshape(1, 1, 2 * KR * KD)


def solution(mesh):
    return jax.shard_map(
        per_device,
        mesh=mesh,
        in_specs=(
            P("dp", "seq", "tensor"),
            P("dp", "seq", None),
            P("tensor", None),
            P(None, "tensor"),
            P("tensor", None),
            P(None, "dp", "tensor"),
            P(None, "dp", "tensor"),
            P(),
            P(),
            P("dp", None, None),
            P("dp", None),
        ),
        out_specs=(P("dp", "seq", "tensor"), P("dp", ("seq", "tensor"), None)),
        check_vma=False,
    )
```

time: 182 us -> 68 us (0.37)
  Pallas kernels: 0 us -> 62.6 us
  waiting for transfers between devices: 62.4 us -> 0 us
  matrix products: 39.3 us -> 0 us
  other arithmetic: 20.6 us -> 0 us
  starting transfers between devices: 20.3 us -> 0 us
  between operations: 17.5 us -> 0.64 us
  local copies, waits for them, and re-layouts: 13.7 us -> 4.49 us
  blocking collectives: 7.17 us -> 0 us
    pallas_call x0 -> x1, Pallas kernels: none -> 62.6 us  [per_device(): pl.pallas_call(kernel, out_shape=(jax.ShapeDtypeStruct((BLK, COLS), bf16)...]
    all_to_all x2 -> x0, waiting for transfers between devices: 41.1 us -> none  [the longest x1 38.2 us: copy_for_each(): lax.all_to_all(jnp.broadcast_to(shard[None], (count, *shard.shape)), axis...]
    dot_general x9 -> x0, matrix products: 39.3 us -> none  [the longest x3 21.7 us: contract_trailing(): lax.dot_general(left, right, (((1,), (1,)), ((), ())), preferred_element_...]
    all_gather x2 -> x0, waiting for transfers between devices: 21.2 us -> none  [the longest x1 21.2 us: carried_in(): lax.all_gather(a.astype(kind), axis)]
    all_to_all x2 -> x0, starting transfers between devices: 20.2 us -> none  [the longest x1 12.1 us: sent_and_summed(): lax.all_to_all(pieces, axis, split_axis=0, concat_axis=0, tiled=True)]
    reduce_sum x5 -> x0, other arithmetic: 12.6 us -> none  [the longest x1 9.85 us: taken_together(): return copy_for_each(shard, axis).sum(axis=0)]
    unnamed x1 -> x0, blocking collectives: 7.17 us -> none
    broadcast_in_dim x2 -> x0, local copies, waits for them, and re-layouts: 4.62 us -> none  [the longest x1 4.62 us: copy_for_each(): jnp.broadcast_to(shard[None], (count, *shard.shape))]
  transfers between devices with their start and end apart: 4 -> 0, of which waited for: 3 -> 0; matrix products, arithmetic and copies ran while one was open for 26% -> 0% of each run, Pallas kernels for 0% -> 0%
where the time goes in v1:
time: 68 us; the launch traced here: 67.8 us
  Pallas kernels  62.6 us (92%)
  local copies, waits for them, and re-layouts  4.49 us (7%)
    pallas_call x1, Pallas kernels, per_device(): pl.pallas_call(kernel, out_shape=(jax.ShapeDtypeStruct((BLK, COLS), bf16)...  62.6 us
    unnamed x1, local copies, waits for them, and re-layouts  3.08 us
    reshape x1, local copies, waits for them, and re-layouts, per_device(): return (att.reshape(1, BLK, COLS), feat.reshape(1, 1, 2 * KR * KD))  1.41 us

profile of v1, /device:TPU:1, one launch (start us, length us, event | category | flops | bytes accessed | tf_op | source)
XLA Modules:
  0.0 67.8 jit_solution(1868501053420842194)
XLA Ops:
  0.6 62.6 %step.1 = (bf16[1024,1024]{1,0:T(8,128)(2,1)}, f32[32,256]{1,0:T(8,128)}) custom-call(bf16[1024,1024]{1,0:T(8,128)(2,1)} %bitcast.5, bf16[1024,4096]{1,0:T(8,128)(2,1)} %bitcast.4, bf16[1024,128]{1,0:T(8,128)(2,1)} %a_hbm.1, bf16[128,1024]{1,0:T(8,128)(2,1)} %b_hbm.1, bf16[1024,4096]{1,0:T(8,128)(2,1)} %w_hbm.1, f32[2,8,1024]{2,1,0:T(8,128)} %m1_hbm.1, ...), custom_call_target="tpu_custom_call" | custom-call | tf_op jit(solution)/shard_map/step/pallas_call | solution.py:425
  63.3 1.4 %reshape.23 = f32[1,1,8192]{2,1,0:T(1,128)} reshape(f32[32,256]{1,0:T(8,128)} %get-tuple-element.5) | data formatting | bytes 65536 | tf_op jit(solution)/shard_map/reshape | solution.py:457
  64.7 3.1 %copy.14 = bf16[1,1024,1024]{2,1,0:T(8,128)(2,1)} copy(bf16[1,1024,1024]{2,1,0:T(8,128)(2,1)} %bitcast.6) | data formatting | bytes 4194304

commit v2 on v1

v2 whole, which is shorter than its diff:
```python
import jax
import jax.numpy as jnp
from jax import lax
from jax.experimental import pallas as pl
from jax.experimental.pallas import tpu as pltpu
from jax.sharding import PartitionSpec as P

TOUCH = 8
SCALE = 4.0
BETA_ONE = 0.9
BETA_TWO = 0.999
EPSILON = 1e-08

N_DP, N_SEQ, N_TP = 16, 4, 4
GROUP = N_SEQ * N_TP
BLK = 1024
WIDTH = 4096
COLS = WIDTH // N_TP
RANK = 128
KR, KD = 16, 256
EX = 16
HALF = BLK // 2
TILE = 256
WIDE = 512
CHUNKS = 4
SIDES = 2
LAG = 2
N_Z = 8
VLIMIT = 60

bf16 = jnp.bfloat16
f32 = jnp.float32
NT = (((1,), (1,)), ((), ()))
MESH_ID = pl.DeviceIdType.MESH


def kernel(
    x_hbm, g_hbm, a_hbm, b_hbm, w_hbm, m1_hbm, m2_hbm, r_hbm, q_hbm, bounds_hbm, owner_hbm,
    out_ref, feat_ref,
    xg, gv, wv, ab, bv, qv, m1v, m2v, rv, bounds, owner, acc,
    ex1s, ex1r, lowh, ex2s, ex2r, low, low_t, parts, cs, cr, mom, uv, facc, fsend, frecv,
    ld_sem, ex_ss, ex_rs, mx_ss, mx_rs, mz_ss, mz_rs, c_ss, c_rs, f_ss, f_rs,
):
    dp = lax.axis_index("dp")
    s = lax.axis_index("seq")
    t = lax.axis_index("tensor")
    core = lax.rem(t, 2)
    chip = lax.div(t, 2)
    partner = chip * 2 + (1 - core)
    across = (1 - chip) * 2 + core
    zi = lax.div(dp, 2)
    xh = lax.rem(dp, 2)
    xpeer = zi * 2 + (1 - xh)
    zright = lax.rem(zi + 1, N_Z)
    zleft = lax.rem(zi + N_Z - 1, N_Z)
    me = s * N_TP + t

    def col(i):
        return pl.ds(pl.multiple_of(lax.rem(t + i, N_TP) * COLS, COLS), COLS)

    def half_rows(h):
        return pl.ds(pl.multiple_of(h * HALF, HALF), HALF)

    def load(i, src, dst):
        return pltpu.make_async_copy(src, dst, ld_sem.at[i])

    ld_b = load(0, b_hbm, bv)
    ld_a = load(1, a_hbm, ab.at[1])
    ld_low = []
    for i, h in enumerate((1 - core, core)):
        ld_low.append(load(2 + 2 * i, g_hbm.at[half_rows(h), col(0)], xg.at[1, half_rows(h), :]))
        ld_low.append(load(3 + 2 * i, x_hbm.at[half_rows(h), :], xg.at[0, half_rows(h), :]))
    ld_m1 = load(6, m1_hbm, m1v)
    ld_m2 = load(7, m2_hbm, m2v)
    ld_g = [load(8 + i, g_hbm.at[:, col(i)], gv.at[:, col(i)]) for i in range(1, N_TP)]
    ld_w = [
        load(12 + i, w_hbm.at[pl.ds(i * WIDE, WIDE), :], wv.at[pl.ds(i * WIDE, WIDE), :])
        for i in range(2)
    ]
    ld_q = load(14, q_hbm.at[col(0), :], qv)
    ld_r = load(15, r_hbm, rv)
    ld_bounds = load(16, bounds_hbm, bounds)
    ld_owner = load(17, owner_hbm, owner)
    own_g = load(8, xg.at[1], gv.at[:, col(0)])
    for c in (ld_b, ld_a, *ld_low, ld_m1, ld_m2, *ld_g, *ld_w, ld_q, ld_r, ld_bounds, ld_owner):
        c.start()

    barrier = pltpu.get_barrier_semaphore()

    def greet(j, _):
        o = lax.rem(me + j, GROUP)
        pl.semaphore_signal(
            barrier, inc=1, device_id={"seq": lax.div(o, N_TP), "tensor": lax.rem(o, N_TP)},
            device_id_type=MESH_ID)
        return 0

    lax.fori_loop(1, GROUP, greet, 0)
    for peer in (xpeer, zright * 2 + xh, zleft * 2 + xh):
        pl.semaphore_signal(barrier, inc=1, device_id={"dp": peer}, device_id_type=MESH_ID)

    def rcopy(src, dst, ss, rs, **where):
        return pltpu.make_async_remote_copy(
            src_ref=src, dst_ref=dst, send_sem=ss, recv_sem=rs, device_id=where,
            device_id_type=MESH_ID)

    ex1 = rcopy(ex1s, ex1r, ex_ss.at[0], ex_rs.at[0], tensor=partner)
    ex2 = rcopy(ex2s, ex2r, ex_ss.at[1], ex_rs.at[1], tensor=across)
    ex3 = rcopy(low.at[core], low.at[core], ex_ss.at[2], ex_rs.at[2], tensor=partner)
    ex3_in = rcopy(low.at[1 - core], low.at[1 - core], ex_ss.at[2], ex_rs.at[2], tensor=partner)

    def mx(m, block):
        return rcopy(mom.at[m, zi, xh], mom.at[m, zi, block], mx_ss.at[m], mx_rs.at[m], dp=xpeer)

    right_dp = zright * 2 + xh
    left_dp = zleft * 2 + xh

    def ring(j, m, ahead):
        zr = lax.rem(zi + N_Z - j - ahead, N_Z)
        zl = lax.rem(zi + j + ahead, N_Z)
        if j < 3:
            a = mom.at[m, zr]
            b = mom.at[m, zl]
        else:
            a = mom.at[m, zr, 0]
            b = mom.at[m, zl, 1]
        return (
            rcopy(a, a, mz_ss.at[j, m, 0], mz_rs.at[j, m, 0], dp=right_dp),
            rcopy(b, b, mz_ss.at[j, m, 1], mz_rs.at[j, m, 1], dp=left_dp),
        )

    def ring_wait(j, m):
        for c in ring(j, m, 1):
            c.wait_recv()

    def ring_step(j, m):
        if j == 0:
            mx(m, 1 - xh).wait_recv()
        else:
            ring_wait(j - 1, m)
        for c in ring(j, m, 0):
            c.start()

    ld_b.wait()
    ab[0] = bv[...].T
    ld_a.wait()

    def partial(i, _):
        m = lax.rem(i, 2)
        late = lax.div(i, 2)
        rows = half_rows(jnp.where(late == 1, core, 1 - core))
        for n in range(4):
            @pl.when(i == n)
            def _():
                ld_low[n].wait()

        p = jnp.dot(xg[1 - m, rows, :], ab[m], preferred_element_type=f32)

        @pl.when(late == 0)
        def _():
            ex1s[m] = p.astype(bf16)

        @pl.when(late == 1)
        def _():
            lowh[m] = p

        @pl.when(i == 1)
        def _():
            pl.semaphore_wait(barrier, GROUP - 1 + 3)
            ex1.start()
            ld_m1.wait()
            ld_m2.wait()
            for mm in range(2):
                mom[mm, zi, xh] = jnp.concatenate([m1v[mm], m2v[mm]], axis=0).astype(bf16)
                mx(mm, xh).start()

        return 0

    lax.fori_loop(0, 4, partial, 0)
    own_g.start()

    for c in ld_g:
        c.wait()
    ld_w[0].wait()
    own_g.wait()

    def main_tile(i, _):
        @pl.when(i == 1)
        def _():
            ex1.wait_recv()
            total = lowh[...] + ex1r[...].astype(f32)
            lowh[...] = total
            ex2s[...] = total.astype(bf16)
            ex2.start()

        @pl.when(i == 2)
        def _():
            ld_w[1].wait()

        @pl.when(i == 3)
        def _():
            ring_step(0, 0)
            ring_step(0, 1)

        rows = half_rows(lax.rem(i, 2))
        cc = pl.ds(pl.multiple_of(lax.div(i, 2) * WIDE, WIDE), WIDE)
        acc[rows, cc] = lax.dot_general(
            gv[rows, :], wv[cc, :], NT, preferred_element_type=f32)
        return 0

    lax.fori_loop(0, 4, main_tile, 0)

    ex2.wait_recv()
    low[core] = (lowh[...] + ex2r[...].astype(f32)).astype(bf16)
    ex3.start()

    ld_bounds.wait()
    ld_owner.wait()
    low_pos = s * BLK
    n_le = jnp.int32(0)
    n_lt = jnp.int32(0)
    n_last = jnp.int32(0)
    n_next = jnp.int32(0)
    pos = low_pos + lax.broadcasted_iota(jnp.int32, (1, BLK), 1)
    ids = jnp.full((1, BLK), -1, jnp.int32)
    for e in range(EX):
        st = bounds[0, e]
        n_le = n_le + (st <= low_pos).astype(jnp.int32)
        n_lt = n_lt + (st < low_pos).astype(jnp.int32)
        n_last = n_last + (st <= low_pos + BLK - 1).astype(jnp.int32)
        n_next = n_next + (st <= low_pos + BLK).astype(jnp.int32)
        ids = ids + (st <= pos).astype(jnp.int32)
    first_id = n_le - 1
    last_id = n_last - 1
    n_slots = last_id - first_id
    single = (first_id == last_id).astype(f32)
    inside = (s < N_SEQ - 1).astype(jnp.int32)
    from_left = (n_le == n_lt).astype(f32)
    from_right = ((n_next == n_last).astype(jnp.int32) * inside).astype(f32)
    begins = (from_left, from_right)
    keeps = (from_left * single, from_right * single)

    def mask_of(side, k):
        slot = jnp.where(side == 0, ids - first_id, last_id - ids)
        return (slot == k).astype(f32).astype(bf16)

    ring_step(1, 0)
    ex3_in.wait_recv()

    def turn(i, _):
        h = lax.div(i, 2)
        m = lax.rem(i, 2)
        rows = pl.ds(pl.multiple_of(m * RANK, RANK), RANK)
        low_t[rows, half_rows(h)] = (low[h, m].astype(f32) * SCALE).T.astype(bf16)
        return 0

    lax.fori_loop(0, 4, turn, 0)

    def rank_rows(m):
        return pl.ds(pl.multiple_of(m * RANK, RANK), RANK)

    def far(i, _):
        m = lax.div(i, 2)
        side = lax.rem(i, 2)
        left = low_t[rank_rows(m), :] * mask_of(side, n_slots)
        p = jnp.dot(left, xg[m, :, half_rows(side)], preferred_element_type=f32).astype(bf16)
        cs[side, 2 * m] = p[:64]
        cs[side, 2 * m + 1] = p[64:]
        return 0

    lax.fori_loop(0, 4, far, 0)

    @pl.when(s == 0)
    def _():
        cr[0] = jnp.zeros((CHUNKS, 64, WIDE), bf16)

    @pl.when(s == N_SEQ - 1)
    def _():
        cr[1] = jnp.zeros((CHUNKS, 64, WIDE), bf16)

    places = (s, N_SEQ - 1 - s)
    nexts = (lax.rem(s + 1, N_SEQ), lax.rem(s + N_SEQ - 1, N_SEQ))

    def chain_copy(d, c):
        return rcopy(cs.at[d, c], cr.at[d, c], c_ss.at[d, c], c_rs.at[d, c], seq=nexts[d])

    def chain(p):
        for d in range(SIDES):
            c = p - LAG * places[d]

            @pl.when((c >= 0) & (c < CHUNKS) & (places[d] < N_SEQ - 1))
            def _():
                @pl.when(places[d] > 0)
                def _():
                    chain_copy(d, c).wait_recv()
                    cs[d, c] = (
                        cs[d, c].astype(f32) + keeps[d] * cr[d, c].astype(f32)).astype(bf16)

                chain_copy(d, c).start()

    chain(0)
    ring_step(1, 1)

    def part_tile(i, _):
        m = lax.div(i, 4)
        side = lax.rem(lax.div(i, 2), 2)
        group = lax.rem(i, 2)

        @pl.when((lax.rem(i, 2) == 0) & (i > 0))
        def _():
            chain(lax.div(i, 2))

        for n, (j, mm) in ((2, (2, 0)), (4, (2, 1)), (7, (3, 0))):
            @pl.when(i == n)
            def _():
                ring_step(j, mm)

        low_m = low_t[rank_rows(m), :]
        left = jnp.concatenate([low_m * mask_of(side, group * 4 + k) for k in range(4)], axis=0)
        p = jnp.dot(left, xg[m, :, half_rows(side)], preferred_element_type=f32)
        parts[m, half_rows(group), half_rows(side)] = p.astype(bf16)
        return 0

    lax.fori_loop(0, 8, part_tile, 0)
    chain(4)
    ring_step(3, 1)

    def fix(i, _):
        rows = pl.ds(pl.multiple_of(i * TILE, TILE), TILE)
        h = lax.div(i, 2)
        sub = pl.ds(pl.multiple_of(lax.rem(i, 2) * TILE, TILE), TILE)
        corr = lax.dot_general(low[h, 0, sub, :], ab[1], NT, preferred_element_type=f32)
        out_ref[rows, :] = (acc[rows, :] + SCALE * corr).astype(bf16)
        return 0

    lax.fori_loop(0, BLK // TILE, fix, 0)
    chain(5)

    ring_wait(3, 0)
    ring_wait(3, 1)
    ld_q.wait()
    ld_r.wait()
    r = rv[...]
    r_hi = r.astype(bf16)
    r_lo = (r - r_hi.astype(f32)).astype(bf16)
    r2 = jnp.concatenate([r_hi, r_lo], axis=0)

    go = []
    for k in range(TOUCH):
        e = jnp.minimum(first_id + k, EX - 1)
        done = (k <= n_slots) & (bounds[1, e] <= low_pos + BLK)
        left_go = jnp.where(done, owner[0, e], -1)
        e = jnp.maximum(last_id - k, 0)
        done = (k <= n_slots) & (bounds[0, e] >= low_pos)
        go.append((left_go, jnp.where(done, owner[0, e], -1)))

    def widths(side, lo, n):
        u = uv[side, lo * 64:(lo + n) * 64, :]
        return jnp.dot(u, qv[side * WIDE:(side + 1) * WIDE, :], preferred_element_type=f32)

    def feature_rows(f):
        return jnp.concatenate([f[:KR] + f[KR:2 * KR], f[2 * KR:3 * KR] + f[3 * KR:]], axis=0)

    def normalized(i, _):
        k = lax.rem(lax.div(i, 2) + 1, TOUCH)
        m = lax.rem(i, 2)
        for n, p in ((4, 6), (8, 7)):
            @pl.when(i == n)
            def _():
                chain(p)

        @pl.when(i == 14)
        def _():
            for d in range(SIDES):
                @pl.when(places[d] == N_SEQ - 1)
                def _():
                    for c in range(CHUNKS):
                        chain_copy(d, c).wait_recv()

            for d in range(SIDES):
                cc = slice(d * WIDE, (d + 1) * WIDE)
                for c in range(CHUNKS):
                    rr = slice((c % 2) * 64, (c % 2) * 64 + 64)
                    parts[c // 2, rr, cc] = (
                        parts[c // 2, rr, cc].astype(f32)
                        + begins[d] * cr[d, c].astype(f32)).astype(bf16)

        for c in range(COLS // TILE):
            cc = slice(c * TILE, (c + 1) * TILE)
            rows = []
            for z in range(N_Z):
                a = mom[m, z, 0, :, cc].astype(f32)
                b = mom[m, z, 1, :, cc].astype(f32)
                m1 = jnp.concatenate([a[:8], b[:8]], axis=0)
                m2 = jnp.concatenate([a[8:], b[8:]], axis=0)
                g = parts[m, pl.ds(pl.multiple_of(k * RANK + z * 16, 16), 16), cc].astype(f32)
                first = BETA_ONE * m1 + (1.0 - BETA_ONE) * g
                second = BETA_TWO * m2 + (1.0 - BETA_TWO) * (g * g)
                root = second * lax.rsqrt(second) + EPSILON
                rows.append((first * lax.rsqrt(root * root)).astype(bf16))
            u = jnp.dot(r2, jnp.concatenate(rows, axis=0), preferred_element_type=f32)
            u = u[:KR] + u[KR:]
            hi = u.astype(bf16)
            side = c // 2
            uc = slice((c % 2) * TILE, (c % 2) * TILE + TILE)
            uv[side, pl.ds(pl.multiple_of(i * 32, 32), 16), uc] = hi
            uv[side, pl.ds(pl.multiple_of(i * 32 + 16, 16), 16), uc] = (
                u - hi.astype(f32)).astype(bf16)
        return 0

    lax.fori_loop(0, 2 * TOUCH, normalized, 0)

    fs = [[None] * TOUCH, [None] * TOUCH]
    for d in range(SIDES):
        f = widths(d, 0, TOUCH)
        for kk in range(TOUCH):
            facc[d, kk] = feature_rows(f[kk * 64:(kk + 1) * 64])

    def place(o, _):
        total = jnp.zeros((2 * KR, KD), f32)
        for k in range(TOUCH):
            for d in range(SIDES):
                total = total + jnp.where(go[k][d] == o, 1.0, 0.0) * facc[d, (k + TOUCH - 1) % TOUCH]
        fsend[o] = total.astype(bf16)
        return 0

    lax.fori_loop(0, GROUP, place, 0)

    def feature_copy(o, j):
        return rcopy(
            fsend.at[o], frecv.at[me], f_ss.at[j], f_rs.at[me],
            seq=lax.div(o, N_TP), tensor=lax.rem(o, N_TP))

    def send_out(j, _):
        feature_copy(lax.rem(me + j, GROUP), j).start()
        return 0

    lax.fori_loop(1, GROUP, send_out, 0)
    frecv[me] = fsend[me]

    def arrive(j, _):
        o = lax.rem(me + j, GROUP)
        rcopy(fsend.at[o], frecv.at[o], f_ss.at[j], f_rs.at[o],
              seq=lax.div(o, N_TP), tensor=lax.rem(o, N_TP)).wait_recv()
        return 0

    lax.fori_loop(1, GROUP, arrive, 0)

    def add(o, total):
        return total + frecv[o].astype(f32)

    feat = lax.fori_loop(0, GROUP, add, jnp.zeros((2 * KR, KD), f32))
    feat_ref[pl.ds(0, 2 * KR, stride=2), :] = feat[:, :128]
    feat_ref[pl.ds(1, 2 * KR, stride=2), :] = feat[:, 128:]

    ex1.wait_send()
    ex2.wait_send()
    ex3.wait_send()
    for m in range(2):
        mx(m, xh).wait_send()
        for j in range(4):
            for c in ring(j, m, 0):
                c.wait_send()

    for d in range(SIDES):
        @pl.when(places[d] < N_SEQ - 1)
        def _():
            for c in range(CHUNKS):
                chain_copy(d, c).wait_send()

    def left(j, _):
        feature_copy(lax.rem(me + j, GROUP), j).wait_send()
        return 0

    lax.fori_loop(1, GROUP, left, 0)


def per_device(x, g, a, b, w, m1, m2, r, q, bounds, owner):
    hbm = pl.BlockSpec(memory_space=pltpu.HBM)
    vmem = pl.BlockSpec(memory_space=pltpu.VMEM)
    dma = pltpu.SemaphoreType.DMA
    V = pltpu.VMEM
    att, feat = pl.pallas_call(
        kernel,
        out_shape=(
            jax.ShapeDtypeStruct((BLK, COLS), bf16),
            jax.ShapeDtypeStruct((4 * KR, KD // 2), f32),
        ),
        in_specs=[hbm] * 11,
        out_specs=(vmem, vmem),
        scratch_shapes=[
            V((2, BLK, COLS), bf16), V((BLK, WIDTH), bf16), V((COLS, WIDTH), bf16),
            V((2, COLS, RANK), bf16), V((RANK, COLS), bf16), V((COLS, KD), bf16),
            V((2, 8, COLS), f32), V((2, 8, COLS), f32), V((KR, RANK), f32),
            pltpu.SMEM((2, EX), jnp.int32), pltpu.SMEM((1, EX), jnp.int32),
            V((BLK, COLS), f32),
            V((2, HALF, RANK), bf16), V((2, HALF, RANK), bf16), V((2, HALF, RANK), f32),
            V((2, HALF, RANK), bf16), V((2, HALF, RANK), bf16),
            V((2, 2, HALF, RANK), bf16), V((2 * RANK, BLK), bf16),
            V((2, TOUCH * RANK, COLS), bf16),
            V((SIDES, CHUNKS, 64, WIDE), bf16), V((SIDES, CHUNKS, 64, WIDE), bf16),
            V((2, N_Z, 2, 16, COLS), bf16),
            V((SIDES, TOUCH * 64, WIDE), bf16), V((SIDES, TOUCH, 2 * KR, KD), f32),
            V((GROUP, 2 * KR, KD), bf16), V((GROUP, 2 * KR, KD), bf16),
            dma((18,)), dma((3,)), dma((3,)), dma((2,)), dma((2,)),
            dma((4, 2, 2)), dma((4, 2, 2)), dma((SIDES, CHUNKS)), dma((SIDES, CHUNKS)),
            dma((GROUP,)), dma((GROUP,)),
        ],
        compiler_params=pltpu.CompilerParams(
            collective_id=0, has_side_effects=True, vmem_limit_bytes=VLIMIT * 2**20),
        name="step",
    )(
        x.reshape(BLK, COLS), g.reshape(BLK, WIDTH), a, b, w, m1, m2, r, q,
        bounds.reshape(2, EX), owner.reshape(1, EX),
    )
    return att.reshape(1, BLK, COLS), feat.reshape(1, 1, 2 * KR * KD)


def solution(mesh):
    return jax.shard_map(
        per_device,
        mesh=mesh,
        in_specs=(
            P("dp", "seq", "tensor"),
            P("dp", "seq", None),
            P("tensor", None),
            P(None, "tensor"),
            P("tensor", None),
            P(None, "dp", "tensor"),
            P(None, "dp", "tensor"),
            P(),
            P(),
            P("dp", None, None),
            P("dp", None),
        ),
        out_specs=(P("dp", "seq", "tensor"), P("dp", ("seq", "tensor"), None)),
        check_vma=False,
    )
```

time: 68 us -> 57.5 us (0.85)
  Pallas kernels: 62.6 us -> 53 us
  local copies, waits for them, and re-layouts: 4.49 us -> 3.7 us
    pallas_call x1, Pallas kernels: 62.6 us -> 53 us  [per_device(): pl.pallas_call(kernel, out_shape=(jax.ShapeDtypeStruct((BLK, COLS), bf16)...]
    reshape x1 -> x0, local copies, waits for them, and re-layouts: 1.41 us -> none  [per_device(): return (att.reshape(1, BLK, COLS), feat.reshape(1, 1, 2 * KR * KD))]
    unnamed x1 -> x4, local copies, waits for them, and re-layouts: 3.08 us -> 3.7 us
where the time goes in v2:
time: 57.5 us; the launch traced here: 57.4 us
  Pallas kernels  53 us (92%)
  local copies, waits for them, and re-layouts  3.7 us (6%)
  between operations  0.65 us (1%)
    pallas_call x1, Pallas kernels, per_device(): pl.pallas_call(kernel, out_shape=(jax.ShapeDtypeStruct((BLK, COLS), bf16)...  53 us
    unnamed x4, local copies, waits for them, and re-layouts  3.7 us

profile of v2, /device:TPU:1, one launch (start us, length us, event | category | flops | bytes accessed | tf_op | source)
XLA Modules:
  0.0 57.4 jit_solution(3286506682151111448)
XLA Ops:
  0.6 53.0 %step.1 = (bf16[1024,1024]{1,0:T(8,128)(2,1)}, f32[64,128]{1,0:T(8,128)}) custom-call(bf16[1024,1024]{1,0:T(8,128)(2,1)} %bitcast.6, bf16[1024,4096]{1,0:T(8,128)(2,1)} %bitcast.5, bf16[1024,128]{1,0:T(8,128)(2,1)} %a_hbm.1, bf16[128,1024]{1,0:T(8,128)(2,1)} %b_hbm.1, bf16[1024,4096]{1,0:T(8,128)(2,1)} %w_hbm.1, f32[2,8,1024]{2,1,0:T(8,128)} %m1_hbm.1, ...), custom_call_target="tpu_custom_call" | custom-call | tf_op jit(solution)/shard_map/step/pallas_call | solution.py:482
  53.7 0.0 copy-start
  53.7 3.1 %copy.15 = bf16[1,1024,1024]{2,1,0:T(8,128)(2,1)} copy(bf16[1,1024,1024]{2,1,0:T(8,128)(2,1)} %bitcast.7) | data formatting | bytes 4194304
  56.8 0.0 copy-done
  56.8 0.6 %copy.16 = f32[1,1,8192]{2,1,0:T(1,128)} copy(f32[1,1,8192]{2,1,0:T(1,128)S(1)} %bitcast.8) | data formatting | bytes 65536
Async XLA Ops:
  53.7 3.1 %copy-start = (f32[64,128]{1,0:T(8,128)S(1)}, f32[64,128]{1,0:T(8,128)}, u32[]{:S(2)}) copy-start(f32[64,128]{1,0:T(8,128)} %get-tuple-element.5) | copy-start | bytes 98308

commit v3 on v2

v3 whole, which is shorter than its diff:
```python
import jax
import jax.numpy as jnp
from jax import lax
from jax.experimental import pallas as pl
from jax.experimental.pallas import tpu as pltpu
from jax.sharding import PartitionSpec as P

TOUCH = 8
SCALE = 4.0
BETA_ONE = 0.9
BETA_TWO = 0.999
EPSILON = 1e-08

N_DP, N_SEQ, N_TP = 16, 4, 4
GROUP = N_SEQ * N_TP
BLK = 1024
WIDTH = 4096
COLS = WIDTH // N_TP
RANK = 128
KR, KD = 16, 256
EX = 16
HALF = BLK // 2
TILE = 256
WIDE = 512
CHUNKS = 4
SIDES = 2
N_Z = 8
VLIMIT = 60

bf16 = jnp.bfloat16
f32 = jnp.float32
NT = (((1,), (1,)), ((), ()))
MESH_ID = pl.DeviceIdType.MESH


def kernel(
    x_hbm, g_hbm, a_hbm, b_hbm, w_hbm, m1_hbm, m2_hbm, r_hbm, q_hbm, bounds_hbm, owner_hbm,
    out_hbm, feat_ref,
    xg, gv, wv, ab, bv, qv, m1v, m2v, rv, bounds, owner, acc, outv,
    ex1s, ex1r, lowh, ex2s, ex2r, low, low_t, parts, cs, cr, mom, uv, fv, facc, fsend, frecv,
    ld_sem, out_sem, ex_ss, ex_rs, mx_ss, mx_rs, mz_ss, mz_rs, c_ss, c_rs, f_ss, f_rs,
):
    dp = lax.axis_index("dp")
    s = lax.axis_index("seq")
    t = lax.axis_index("tensor")
    core = lax.rem(t, 2)
    chip = lax.div(t, 2)
    partner = chip * 2 + (1 - core)
    across = (1 - chip) * 2 + core
    zi = lax.div(dp, 2)
    xh = lax.rem(dp, 2)
    xpeer = zi * 2 + (1 - xh)
    zright = lax.rem(zi + 1, N_Z)
    zleft = lax.rem(zi + N_Z - 1, N_Z)
    me = s * N_TP + t

    def col(i):
        return pl.ds(pl.multiple_of(lax.rem(t + i, N_TP) * COLS, COLS), COLS)

    def half_rows(h):
        return pl.ds(pl.multiple_of(h * HALF, HALF), HALF)

    def load(i, src, dst):
        return pltpu.make_async_copy(src, dst, ld_sem.at[i])

    ld_m1 = load(0, m1_hbm, m1v)
    ld_m2 = load(1, m2_hbm, m2v)
    ld_a = load(2, a_hbm, ab.at[1])
    ld_b = load(3, b_hbm, bv)
    ld_low = [
        load(4 + i, x_hbm.at[half_rows(h), :], xg.at[0, half_rows(h), :])
        for i, h in enumerate((1 - core, core))
    ] + [
        load(6 + i, g_hbm.at[half_rows(h), col(0)], xg.at[1, half_rows(h), :])
        for i, h in enumerate((1 - core, core))
    ]
    ld_g = [
        [load(8 + 4 * h + i, g_hbm.at[half_rows(h), col(i)], gv.at[half_rows(h), col(i)])
         for i in range(1, N_TP)] for h in range(2)
    ]
    own_g = [load(8 + 4 * h, xg.at[1, half_rows(h), :], gv.at[half_rows(h), col(0)])
             for h in range(2)]
    ld_w = [
        load(16 + i, w_hbm.at[pl.ds(i * WIDE, WIDE), :], wv.at[pl.ds(i * WIDE, WIDE), :])
        for i in range(2)
    ]
    ld_q = load(18, q_hbm.at[col(0), :], qv)
    ld_r = load(19, r_hbm, rv)
    ld_bounds = load(20, bounds_hbm, bounds)
    ld_owner = load(21, owner_hbm, owner)
    for c in (ld_m1, ld_m2, ld_a, ld_low[0], ld_low[1], ld_b, ld_low[2], ld_low[3], *ld_g[0],
              ld_w[0], *ld_g[1], ld_w[1], ld_q, ld_r, ld_bounds, ld_owner):
        c.start()

    barrier = pltpu.get_barrier_semaphore()

    def greet(j, _):
        o = lax.rem(me + j, GROUP)
        pl.semaphore_signal(
            barrier, inc=1, device_id={"seq": lax.div(o, N_TP), "tensor": lax.rem(o, N_TP)},
            device_id_type=MESH_ID)
        return 0

    lax.fori_loop(1, GROUP, greet, 0)
    for peer in (xpeer, zright * 2 + xh, zleft * 2 + xh):
        pl.semaphore_signal(barrier, inc=1, device_id={"dp": peer}, device_id_type=MESH_ID)

    def rcopy(src, dst, ss, rs, **where):
        return pltpu.make_async_remote_copy(
            src_ref=src, dst_ref=dst, send_sem=ss, recv_sem=rs, device_id=where,
            device_id_type=MESH_ID)

    def ex1(m):
        return rcopy(ex1s.at[m], ex1r.at[m], ex_ss.at[0, m], ex_rs.at[0, m], tensor=partner)

    def ex2(m):
        return rcopy(ex2s.at[m], ex2r.at[m], ex_ss.at[1, m], ex_rs.at[1, m], tensor=across)

    def ex3(m, half):
        return rcopy(low.at[half, m], low.at[half, m], ex_ss.at[2, m], ex_rs.at[2, m],
                     tensor=partner)

    def second(m):
        ex1(m).wait_recv()
        total = lowh[m] + ex1r[m].astype(f32)
        lowh[m] = total
        ex2s[m] = total.astype(bf16)
        ex2(m).start()

    def third(m):
        ex2(m).wait_recv()
        low[core, m] = (lowh[m] + ex2r[m].astype(f32)).astype(bf16)
        ex3(m, core).start()

    def mx(m, block):
        return rcopy(mom.at[m, zi, xh], mom.at[m, zi, block], mx_ss.at[m], mx_rs.at[m], dp=xpeer)

    right_dp = zright * 2 + xh
    left_dp = zleft * 2 + xh

    def ring(j, m, ahead):
        zr = lax.rem(zi + N_Z - j - ahead, N_Z)
        zl = lax.rem(zi + j + ahead, N_Z)
        if j < 3:
            a = mom.at[m, zr]
            b = mom.at[m, zl]
        else:
            a = mom.at[m, zr, 0]
            b = mom.at[m, zl, 1]
        return (
            rcopy(a, a, mz_ss.at[j, m, 0], mz_rs.at[j, m, 0], dp=right_dp),
            rcopy(b, b, mz_ss.at[j, m, 1], mz_rs.at[j, m, 1], dp=left_dp),
        )

    def ring_wait(j, m):
        for c in ring(j, m, 1):
            c.wait_recv()

    def ring_step(j, m):
        if j == 0:
            mx(m, 1 - xh).wait_recv()
        else:
            ring_wait(j - 1, m)
        for c in ring(j, m, 0):
            c.start()

    ld_a.wait()

    def partial(i, _):
        m = 1 - lax.div(i, 2)
        late = lax.rem(i, 2)
        rows = half_rows(jnp.where(late == 1, core, 1 - core))

        @pl.when(i == 2)
        def _():
            ld_b.wait()
            ab[0] = bv[...].T

        for n in range(4):
            @pl.when(i == n)
            def _():
                ld_low[n].wait()

        p = jnp.dot(xg[1 - m, rows, :], ab[m], preferred_element_type=f32)

        @pl.when(late == 0)
        def _():
            ex1s[m] = p.astype(bf16)

        @pl.when(late == 1)
        def _():
            lowh[m] = p

        @pl.when(i == 0)
        def _():
            pl.semaphore_wait(barrier, GROUP - 1 + 3)
            ex1(1).start()
            ld_m1.wait()
            ld_m2.wait()
            for mm in range(2):
                mom[mm, zi, xh] = jnp.concatenate([m1v[mm], m2v[mm]], axis=0).astype(bf16)
                mx(mm, xh).start()

        @pl.when(i == 2)
        def _():
            ex1(0).start()

        return 0

    lax.fori_loop(0, 4, partial, 0)
    for c in own_g:
        c.start()
    second(1)

    for c in ld_g[0]:
        c.wait()
    own_g[0].wait()
    ld_w[0].wait()
    second(0)

    def main_tile(i, _):
        @pl.when(i == 1)
        def _():
            for c in ld_g[1]:
                c.wait()
            own_g[1].wait()
            ring_step(0, 0)
            ring_step(0, 1)

        @pl.when(i == 2)
        def _():
            ld_w[1].wait()
            third(1)

        rows = half_rows(lax.rem(i, 2))
        cc = pl.ds(pl.multiple_of(lax.div(i, 2) * WIDE, WIDE), WIDE)
        acc[rows, cc] = lax.dot_general(
            gv[rows, :], wv[cc, :], NT, preferred_element_type=f32)
        return 0

    lax.fori_loop(0, 3, main_tile, 0)

    third(0)
    ring_step(1, 0)

    ld_bounds.wait()
    ld_owner.wait()
    low_pos = s * BLK
    n_le = jnp.int32(0)
    n_lt = jnp.int32(0)
    n_last = jnp.int32(0)
    n_next = jnp.int32(0)
    pos = low_pos + lax.broadcasted_iota(jnp.int32, (1, BLK), 1)
    ids = jnp.full((1, BLK), -1, jnp.int32)
    for e in range(EX):
        st = bounds[0, e]
        n_le = n_le + (st <= low_pos).astype(jnp.int32)
        n_lt = n_lt + (st < low_pos).astype(jnp.int32)
        n_last = n_last + (st <= low_pos + BLK - 1).astype(jnp.int32)
        n_next = n_next + (st <= low_pos + BLK).astype(jnp.int32)
        ids = ids + (st <= pos).astype(jnp.int32)
    first_id = n_le - 1
    last_id = n_last - 1
    n_slots = last_id - first_id
    single = (first_id == last_id).astype(f32)
    inside = (s < N_SEQ - 1).astype(jnp.int32)
    from_left = (n_le == n_lt).astype(f32)
    from_right = ((n_next == n_last).astype(jnp.int32) * inside).astype(f32)
    begins = (from_left, from_right)
    keeps = (from_left * single, from_right * single)

    def mask_of(side, k):
        slot = jnp.where(side == 0, ids - first_id, last_id - ids)
        return (slot == k).astype(f32).astype(bf16)

    def rank_rows(m):
        return pl.ds(pl.multiple_of(m * RANK, RANK), RANK)

    places = (s, N_SEQ - 1 - s)
    nexts = (lax.rem(s + 1, N_SEQ), lax.rem(s + N_SEQ - 1, N_SEQ))

    def chain_copy(d, c):
        return rcopy(cs.at[d, c], cr.at[d, c], c_ss.at[d, c], c_rs.at[d, c], seq=nexts[d])

    def chain(place, c):
        for d in range(SIDES):
            @pl.when(places[d] == place)
            def _():
                if place > 0:
                    chain_copy(d, c).wait_recv()
                    cs[d, c] = (
                        cs[d, c].astype(f32) + keeps[d] * cr[d, c].astype(f32)).astype(bf16)
                chain_copy(d, c).start()

    def far(i, _):
        m = 1 - lax.div(i, 2)
        side = lax.rem(i, 2)

        for mm in (1, 0):
            @pl.when(i == 2 * (1 - mm))
            def _():
                if mm == 0:
                    chain(0, 0)
                    chain(0, 1)
                    ring_step(1, 1)
                ex3(mm, 1 - core).wait_recv()

        @pl.when(side == 0)
        def _():
            for h in range(2):
                low_t[rank_rows(m), h * HALF:(h + 1) * HALF] = (
                    low[h, m].astype(f32) * SCALE).T.astype(bf16)

        left = low_t[rank_rows(m), :] * mask_of(side, n_slots)
        p = jnp.dot(left, xg[m, :, half_rows(side)], preferred_element_type=f32).astype(bf16)
        cs[side, 2 - 2 * m] = p[:64]
        cs[side, 3 - 2 * m] = p[64:]
        return 0

    lax.fori_loop(0, 4, far, 0)
    chain(0, 2)
    chain(0, 3)

    @pl.when(s == 0)
    def _():
        cr[0] = jnp.zeros((CHUNKS, 64, WIDE), bf16)

    @pl.when(s == N_SEQ - 1)
    def _():
        cr[1] = jnp.zeros((CHUNKS, 64, WIDE), bf16)

    def part_tile(i, _):
        m = lax.div(i, 4)
        side = lax.rem(lax.div(i, 2), 2)
        group = lax.rem(i, 2)

        for n, steps in (
            (1, ((2, 0),)), (4, ((2, 1),)), (6, ((3, 0),)),
        ):
            @pl.when(i == n)
            def _():
                for j, mm in steps:
                    ring_step(j, mm)

        for n, steps in (
            (3, ((1, 0),)), (5, ((1, 1),)), (7, ((1, 2), (2, 0))),
        ):
            @pl.when(i == n)
            def _():
                for place, c in steps:
                    chain(place, c)

        low_m = low_t[rank_rows(m), :]
        left = jnp.concatenate([low_m * mask_of(side, group * 4 + k) for k in range(4)], axis=0)
        p = jnp.dot(left, xg[m, :, half_rows(side)], preferred_element_type=f32)
        parts[m, half_rows(group), half_rows(side)] = p.astype(bf16)
        return 0

    lax.fori_loop(0, 8, part_tile, 0)
    ring_step(3, 1)

    ld_q.wait()
    ld_r.wait()
    ring_wait(3, 0)
    r = rv[...]
    r_hi = r.astype(bf16)
    r_lo = (r - r_hi.astype(f32)).astype(bf16)
    r2 = jnp.concatenate([r_hi, r_lo], axis=0)

    go = []
    for k in range(TOUCH):
        e = jnp.minimum(first_id + k, EX - 1)
        done = (k <= n_slots) & (bounds[1, e] <= low_pos + BLK)
        left_go = jnp.where(done, owner[0, e], -1)
        e = jnp.maximum(last_id - k, 0)
        done = (k <= n_slots) & (bounds[0, e] >= low_pos)
        go.append((left_go, jnp.where(done, owner[0, e], -1)))

    def widths(side, lo, n):
        u = uv[side, lo * 64:(lo + n) * 64, :]
        f = jnp.dot(u, qv[side * WIDE:(side + 1) * WIDE, :], preferred_element_type=f32)
        for i in range(n):
            v = f[i * 64:(i + 1) * 64]
            fv[side, lo + i] = jnp.concatenate(
                [v[:KR] + v[KR:2 * KR], v[2 * KR:3 * KR] + v[3 * KR:]], axis=0)

    def placed(o, total, slots):
        for k in slots:
            for d in range(SIDES):
                total = total + jnp.where(go[k][d] == o, 1.0, 0.0) * fv[d, (k + TOUCH - 1) % TOUCH]
        return total

    def normalized(i, _):
        early = i < 2 * (TOUCH - 1)
        m = jnp.where(early, lax.div(i, TOUCH - 1), i - 2 * (TOUCH - 1))
        k = jnp.where(early, lax.rem(i, TOUCH - 1) + 1, 0)
        row = jnp.where(early, k - 1, TOUCH - 1) * 64 + m * 32
        for n, steps in (
            (0, ((1, 3), (2, 1))), (3, ((2, 2),)), (6, ((2, 3),)),
        ):
            @pl.when(i == n)
            def _():
                for place, c in steps:
                    chain(place, c)

        @pl.when(i == TOUCH - 1)
        def _():
            ring_wait(3, 1)

        @pl.when(i == 2 * (TOUCH - 1))
        def _():
            for d in range(SIDES):
                widths(d, 0, TOUCH - 1)

            def place_most(o, _):
                facc[o] = placed(o, jnp.zeros((2 * KR, KD), f32), range(1, TOUCH))
                return 0

            lax.fori_loop(0, GROUP, place_most, 0)
            for d in range(SIDES):
                @pl.when(places[d] == N_SEQ - 1)
                def _():
                    for c in range(CHUNKS):
                        chain_copy(d, c).wait_recv()

            for d in range(SIDES):
                cc = slice(d * WIDE, (d + 1) * WIDE)
                for c in range(CHUNKS):
                    rr = slice((c % 2) * 64, (c % 2) * 64 + 64)
                    parts[1 - c // 2, rr, cc] = (
                        parts[1 - c // 2, rr, cc].astype(f32)
                        + begins[d] * cr[d, c].astype(f32)).astype(bf16)

        for c in range(COLS // TILE):
            cc = slice(c * TILE, (c + 1) * TILE)
            rows = []
            for z in range(N_Z):
                a = mom[m, z, 0, :, cc].astype(f32)
                b = mom[m, z, 1, :, cc].astype(f32)
                m1 = jnp.concatenate([a[:8], b[:8]], axis=0)
                m2 = jnp.concatenate([a[8:], b[8:]], axis=0)
                g = parts[m, pl.ds(pl.multiple_of(k * RANK + z * 16, 16), 16), cc].astype(f32)
                first = BETA_ONE * m1 + (1.0 - BETA_ONE) * g
                second = BETA_TWO * m2 + (1.0 - BETA_TWO) * (g * g)
                root = second * lax.rsqrt(second) + EPSILON
                rows.append((first * lax.rsqrt(root * root)).astype(bf16))
            u = jnp.dot(r2, jnp.concatenate(rows, axis=0), preferred_element_type=f32)
            u = u[:KR] + u[KR:]
            hi = u.astype(bf16)
            side = c // 2
            uc = slice((c % 2) * TILE, (c % 2) * TILE + TILE)
            uv[side, pl.ds(pl.multiple_of(row, 32), 16), uc] = hi
            uv[side, pl.ds(pl.multiple_of(row + 16, 16), 16), uc] = (
                u - hi.astype(f32)).astype(bf16)
        return 0

    lax.fori_loop(0, 2 * TOUCH, normalized, 0)

    for d in range(SIDES):
        widths(d, TOUCH - 1, 1)

    def feature_copy(o):
        return rcopy(
            fsend.at[o], frecv.at[me], f_ss.at[o], f_rs.at[me],
            seq=lax.div(o, N_TP), tensor=lax.rem(o, N_TP))

    def place(j, _):
        o = lax.rem(me + 1 + j, GROUP)
        fsend[o] = placed(o, facc[o], (0,)).astype(bf16)

        @pl.when(j < GROUP - 1)
        def _():
            feature_copy(o).start()

        return 0

    lax.fori_loop(0, GROUP, place, 0)
    frecv[me] = fsend[me]

    lax.fori_loop(3, 4, main_tile, 0)

    def out_copy(i):
        rows = pl.ds(pl.multiple_of(i * TILE, TILE), TILE)
        return pltpu.make_async_copy(outv.at[rows, :], out_hbm.at[rows, :], out_sem.at[i])

    def fix(i, _):
        rows = pl.ds(pl.multiple_of(i * TILE, TILE), TILE)
        h = lax.div(i, 2)
        sub = pl.ds(pl.multiple_of(lax.rem(i, 2) * TILE, TILE), TILE)
        corr = lax.dot_general(low[h, 0, sub, :], ab[1], NT, preferred_element_type=f32)
        outv[rows, :] = (acc[rows, :] + SCALE * corr).astype(bf16)
        out_copy(i).start()
        return 0

    lax.fori_loop(0, BLK // TILE, fix, 0)

    def arrive(j, _):
        o = lax.rem(me + j, GROUP)
        rcopy(fsend.at[o], frecv.at[o], f_ss.at[o], f_rs.at[o],
              seq=lax.div(o, N_TP), tensor=lax.rem(o, N_TP)).wait_recv()
        return 0

    lax.fori_loop(1, GROUP, arrive, 0)

    def add(o, total):
        return total + frecv[o].astype(f32)

    feat = lax.fori_loop(0, GROUP, add, jnp.zeros((2 * KR, KD), f32))
    feat_ref[pl.ds(0, 2 * KR, stride=2), :] = feat[:, :128]
    feat_ref[pl.ds(1, 2 * KR, stride=2), :] = feat[:, 128:]

    for m in range(2):
        ex1(m).wait_send()
        ex2(m).wait_send()
        ex3(m, core).wait_send()
        mx(m, xh).wait_send()
        for j in range(4):
            for c in ring(j, m, 0):
                c.wait_send()

    for d in range(SIDES):
        @pl.when(places[d] < N_SEQ - 1)
        def _():
            for c in range(CHUNKS):
                chain_copy(d, c).wait_send()

    def left(j, _):
        feature_copy(lax.rem(me + j, GROUP)).wait_send()
        return 0

    lax.fori_loop(1, GROUP, left, 0)
    for i in range(BLK // TILE):
        out_copy(i).wait()


def per_device(x, g, a, b, w, m1, m2, r, q, bounds, owner):
    any_ = pl.BlockSpec(memory_space=pl.ANY)
    vmem = pl.BlockSpec(memory_space=pltpu.VMEM)
    dma = pltpu.SemaphoreType.DMA
    V = pltpu.VMEM
    att, feat = pl.pallas_call(
        kernel,
        out_shape=(
            jax.ShapeDtypeStruct((BLK, COLS), bf16),
            jax.ShapeDtypeStruct((4 * KR, KD // 2), f32),
        ),
        in_specs=[any_] * 11,
        out_specs=(any_, vmem),
        scratch_shapes=[
            V((2, BLK, COLS), bf16), V((BLK, WIDTH), bf16), V((COLS, WIDTH), bf16),
            V((2, COLS, RANK), bf16), V((RANK, COLS), bf16), V((COLS, KD), bf16),
            V((2, 8, COLS), f32), V((2, 8, COLS), f32), V((KR, RANK), f32),
            pltpu.SMEM((2, EX), jnp.int32), pltpu.SMEM((1, EX), jnp.int32),
            V((BLK, COLS), f32), V((BLK, COLS), bf16),
            V((2, HALF, RANK), bf16), V((2, HALF, RANK), bf16), V((2, HALF, RANK), f32),
            V((2, HALF, RANK), bf16), V((2, HALF, RANK), bf16),
            V((2, 2, HALF, RANK), bf16), V((2 * RANK, BLK), bf16),
            V((2, TOUCH * RANK, COLS), bf16),
            V((SIDES, CHUNKS, 64, WIDE), bf16), V((SIDES, CHUNKS, 64, WIDE), bf16),
            V((2, N_Z, 2, 16, COLS), bf16),
            V((SIDES, TOUCH * 64, WIDE), bf16), V((SIDES, TOUCH, 2 * KR, KD), f32),
            V((GROUP, 2 * KR, KD), f32),
            V((GROUP, 2 * KR, KD), bf16), V((GROUP, 2 * KR, KD), bf16),
            dma((22,)), dma((4,)), dma((3, 2)), dma((3, 2)), dma((2,)), dma((2,)),
            dma((4, 2, 2)), dma((4, 2, 2)), dma((SIDES, CHUNKS)), dma((SIDES, CHUNKS)),
            dma((GROUP,)), dma((GROUP,)),
        ],
        compiler_params=pltpu.CompilerParams(
            collective_id=0, has_side_effects=True, vmem_limit_bytes=VLIMIT * 2**20),
        name="step",
    )(
        x.reshape(BLK, COLS), g.reshape(BLK, WIDTH), a, b, w, m1, m2, r, q,
        bounds.reshape(2, EX), owner.reshape(1, EX),
    )
    return att.reshape(1, BLK, COLS), feat.reshape(1, 1, 2 * KR * KD)


def solution(mesh):
    return jax.shard_map(
        per_device,
        mesh=mesh,
        in_specs=(
            P("dp", "seq", "tensor"),
            P("dp", "seq", None),
            P("tensor", None),
            P(None, "tensor"),
            P("tensor", None),
            P(None, "dp", "tensor"),
            P(None, "dp", "tensor"),
            P(),
            P(),
            P("dp", None, None),
            P("dp", None),
        ),
        out_specs=(P("dp", "seq", "tensor"), P("dp", ("seq", "tensor"), None)),
        check_vma=False,
    )
```

time: 57.5 us -> 52.4 us (0.911)
  Pallas kernels: 53 us -> 47.9 us
    pallas_call x1, Pallas kernels: 53 us -> 47.9 us  [per_device(): pl.pallas_call(kernel, out_shape=(jax.ShapeDtypeStruct((BLK, COLS), bf16)...]
where the time goes in v3:
time: 52.4 us; the launch traced here: 52.3 us
  Pallas kernels  47.9 us (91%)
  local copies, waits for them, and re-layouts  3.7 us (7%)
  between operations  0.65 us (1%)
    pallas_call x1, Pallas kernels, per_device(): pl.pallas_call(kernel, out_shape=(jax.ShapeDtypeStruct((BLK, COLS), bf16)...  47.9 us
    unnamed x4, local copies, waits for them, and re-layouts  3.7 us

profile of v3, /device:TPU:1, one launch (start us, length us, event | category | flops | bytes accessed | tf_op | source)
XLA Modules:
  0.0 52.3 jit_solution(17968042442184522726)
XLA Ops:
  0.6 47.9 %step.1 = (bf16[1024,1024]{1,0:T(8,128)(2,1)}, f32[64,128]{1,0:T(8,128)}) custom-call(bf16[1024,1024]{1,0:T(8,128)(2,1)} %bitcast.6, bf16[1024,4096]{1,0:T(8,128)(2,1)} %bitcast.5, bf16[1024,128]{1,0:T(8,128)(2,1)} %a_hbm.1, bf16[128,1024]{1,0:T(8,128)(2,1)} %b_hbm.1, bf16[1024,4096]{1,0:T(8,128)(2,1)} %w_hbm.1, f32[2,8,1024]{2,1,0:T(8,128)} %m1_hbm.1, ...), custom_call_target="tpu_custom_call" | custom-call | tf_op jit(solution)/shard_map/step/pallas_call | solution.py:541
  48.6 0.0 copy-start
  48.6 3.1 %copy.15 = bf16[1,1024,1024]{2,1,0:T(8,128)(2,1)} copy(bf16[1,1024,1024]{2,1,0:T(8,128)(2,1)} %bitcast.7) | data formatting | bytes 4194304
  51.7 0.0 copy-done
  51.7 0.6 %copy.16 = f32[1,1,8192]{2,1,0:T(1,128)} copy(f32[1,1,8192]{2,1,0:T(1,128)S(1)} %bitcast.8) | data formatting | bytes 65536
Async XLA Ops:
  48.6 3.1 %copy-start = (f32[64,128]{1,0:T(8,128)S(1)}, f32[64,128]{1,0:T(8,128)}, u32[]{:S(2)}) copy-start(f32[64,128]{1,0:T(8,128)} %get-tuple-element.5) | copy-start | bytes 98308

commit v4 on v3

--- a/solution.py
+++ b/solution.py
@@ -22,10 +22,12 @@
 HALF = BLK // 2
 TILE = 256
 WIDE = 512
-CHUNKS = 4
+CHUNKS = 8
+SLICE = 32
 SIDES = 2
 N_Z = 8
 VLIMIT = 60
+PIECES = 8
 
 bf16 = jnp.bfloat16
 f32 = jnp.float32
@@ -35,10 +37,10 @@
 
 def kernel(
     x_hbm, g_hbm, a_hbm, b_hbm, w_hbm, m1_hbm, m2_hbm, r_hbm, q_hbm, bounds_hbm, owner_hbm,
-    out_hbm, feat_ref,
+    out_hbm, frecv,
     xg, gv, wv, ab, bv, qv, m1v, m2v, rv, bounds, owner, acc, outv,
-    ex1s, ex1r, lowh, ex2s, ex2r, low, low_t, parts, cs, cr, mom, uv, fv, facc, fsend, frecv,
-    ld_sem, out_sem, ex_ss, ex_rs, mx_ss, mx_rs, mz_ss, mz_rs, c_ss, c_rs, f_ss, f_rs,
+    ex1s, ex1r, lowh, ex2s, ex2r, low, low_t, parts, cs, cr, mom, scaled, uv, fv, facc, fsend,
+    ld_sem, out_sem, ex_ss, ex_rs, mx_ss, mx_rs, za_ss, za_rs, zb_ss, zb_rs, c_ss, c_rs, f_ss, f_rs,
 ):
     dp = lax.axis_index("dp")
     s = lax.axis_index("seq")
@@ -50,8 +52,8 @@
     zi = lax.div(dp, 2)
     xh = lax.rem(dp, 2)
     xpeer = zi * 2 + (1 - xh)
-    zright = lax.rem(zi + 1, N_Z)
-    zleft = lax.rem(zi + N_Z - 1, N_Z)
+    z_steps = (1, 2, N_Z - 1, N_Z - 2)
+    z_peers = [lax.rem(zi + d, N_Z) * 2 + xh for d in z_steps]
     me = s * N_TP + t
 
     def col(i):
@@ -84,12 +86,12 @@
         load(16 + i, w_hbm.at[pl.ds(i * WIDE, WIDE), :], wv.at[pl.ds(i * WIDE, WIDE), :])
         for i in range(2)
     ]
-    ld_q = load(18, q_hbm.at[col(0), :], qv)
-    ld_r = load(19, r_hbm, rv)
-    ld_bounds = load(20, bounds_hbm, bounds)
-    ld_owner = load(21, owner_hbm, owner)
+    ld_q = load(20, q_hbm.at[col(0), :], qv)
+    ld_r = load(21, r_hbm, rv)
+    ld_bounds = load(22, bounds_hbm, bounds)
+    ld_owner = load(23, owner_hbm, owner)
     for c in (ld_m1, ld_m2, ld_a, ld_low[0], ld_low[1], ld_b, ld_low[2], ld_low[3], *ld_g[0],
-              ld_w[0], *ld_g[1], ld_w[1], ld_q, ld_r, ld_bounds, ld_owner):
+              ld_w[0], *ld_g[1], *ld_w[1:], ld_q, ld_r, ld_bounds, ld_owner):
         c.start()
 
     barrier = pltpu.get_barrier_semaphore()
@@ -102,7 +104,7 @@
         return 0
 
     lax.fori_loop(1, GROUP, greet, 0)
-    for peer in (xpeer, zright * 2 + xh, zleft * 2 + xh):
+    for peer in (xpeer, *z_peers):
         pl.semaphore_signal(barrier, inc=1, device_id={"dp": peer}, device_id_type=MESH_ID)
 
     def rcopy(src, dst, ss, rs, **where):
@@ -132,37 +134,47 @@
         low[core, m] = (lowh[m] + ex2r[m].astype(f32)).astype(bf16)
         ex3(m, core).start()
 
-    def mx(m, block):
-        return rcopy(mom.at[m, zi, xh], mom.at[m, zi, block], mx_ss.at[m], mx_rs.at[m], dp=xpeer)
-
-    right_dp = zright * 2 + xh
-    left_dp = zleft * 2 + xh
-
-    def ring(j, m, ahead):
-        zr = lax.rem(zi + N_Z - j - ahead, N_Z)
-        zl = lax.rem(zi + j + ahead, N_Z)
-        if j < 3:
-            a = mom.at[m, zr]
-            b = mom.at[m, zl]
-        else:
-            a = mom.at[m, zr, 0]
-            b = mom.at[m, zl, 1]
-        return (
-            rcopy(a, a, mz_ss.at[j, m, 0], mz_rs.at[j, m, 0], dp=right_dp),
-            rcopy(b, b, mz_ss.at[j, m, 1], mz_rs.at[j, m, 1], dp=left_dp),
-        )
-
-    def ring_wait(j, m):
-        for c in ring(j, m, 1):
-            c.wait_recv()
-
-    def ring_step(j, m):
-        if j == 0:
-            mx(m, 1 - xh).wait_recv()
-        else:
-            ring_wait(j - 1, m)
-        for c in ring(j, m, 0):
-            c.start()
+    sides_x = (xh, 1 - xh)
+
+    def mx(x):
+        return rcopy(mom.at[zi, xh], mom.at[zi, x], mx_ss, mx_rs, dp=xpeer)
+
+    def near_copy(a, i):
+        block = mom.at[zi, sides_x[a]]
+        return rcopy(block, block, za_ss.at[a, i], za_rs.at[a, i], dp=z_peers[i])
+
+    def near_wait(a, i):
+        block = mom.at[lax.rem(zi + N_Z - z_steps[i], N_Z), sides_x[a]]
+        rcopy(block, block, za_ss.at[a, i], za_rs.at[a, i], dp=z_peers[i]).wait_recv()
+
+    def far_block(a, i, hops):
+        d = z_steps[i] if i < 2 else z_steps[i] - N_Z
+        side = 1 if d > 0 else -1
+        z = lax.rem(zi + 2 * N_Z - side * hops, N_Z)
+        x = sides_x[a]
+        if d in (1, -1):
+            return mom.at[z, x]
+        return mom.at[z, x, 0 if d > 0 else 1]
+
+    def far_copy(a, i):
+        block = far_block(a, i, 2)
+        return rcopy(block, block, zb_ss.at[a, i], zb_rs.at[a, i], dp=z_peers[i])
+
+    def far_wait(a, i):
+        block = far_block(a, i, 3 + i % 2)
+        rcopy(block, block, zb_ss.at[a, i], zb_rs.at[a, i], dp=z_peers[i]).wait_recv()
+
+    def round_one(a):
+        if a == 1:
+            mx(1 - xh).wait_recv()
+        for i in range(4):
+            near_copy(a, i).start()
+
+    def round_two(a):
+        for i in (1, 3):
+            near_wait(a, i)
+        for i in range(4):
+            far_copy(a, i).start()
 
     ld_a.wait()
 
@@ -193,13 +205,14 @@
 
         @pl.when(i == 0)
         def _():
-            pl.semaphore_wait(barrier, GROUP - 1 + 3)
+            pl.semaphore_wait(barrier, GROUP - 1 + 5)
             ex1(1).start()
             ld_m1.wait()
             ld_m2.wait()
             for mm in range(2):
-                mom[mm, zi, xh] = jnp.concatenate([m1v[mm], m2v[mm]], axis=0).astype(bf16)
-                mx(mm, xh).start()
+                mom[zi, xh, mm] = jnp.concatenate([m1v[mm], m2v[mm]], axis=0).astype(bf16)
+            mx(xh).start()
+            round_one(0)
 
         @pl.when(i == 2)
         def _():
@@ -224,13 +237,16 @@
             for c in ld_g[1]:
                 c.wait()
             own_g[1].wait()
-            ring_step(0, 0)
-            ring_step(0, 1)
+
+        @pl.when(i == 1)
+        def _():
+            round_one(1)
 
         @pl.when(i == 2)
         def _():
             ld_w[1].wait()
             third(1)
+            round_two(0)
 
         rows = half_rows(lax.rem(i, 2))
         cc = pl.ds(pl.multiple_of(lax.div(i, 2) * WIDE, WIDE), WIDE)
@@ -241,7 +257,6 @@
     lax.fori_loop(0, 3, main_tile, 0)
 
     third(0)
-    ring_step(1, 0)
 
     ld_bounds.wait()
     ld_owner.wait()
@@ -300,9 +315,8 @@
             @pl.when(i == 2 * (1 - mm))
             def _():
                 if mm == 0:
-                    chain(0, 0)
-                    chain(0, 1)
-                    ring_step(1, 1)
+                    for c in range(CHUNKS // 2):
+                        chain(0, c)
                 ex3(mm, 1 - core).wait_recv()
 
         @pl.when(side == 0)
@@ -313,21 +327,22 @@
 
         left = low_t[rank_rows(m), :] * mask_of(side, n_slots)
         p = jnp.dot(left, xg[m, :, half_rows(side)], preferred_element_type=f32).astype(bf16)
-        cs[side, 2 - 2 * m] = p[:64]
-        cs[side, 3 - 2 * m] = p[64:]
+        for c in range(CHUNKS // 2):
+            cs[side, (1 - m) * (CHUNKS // 2) + c] = p[c * SLICE:(c + 1) * SLICE]
         return 0
 
     lax.fori_loop(0, 4, far, 0)
-    chain(0, 2)
-    chain(0, 3)
+    for c in range(CHUNKS // 2, CHUNKS):
+        chain(0, c)
+    round_two(1)
 
     @pl.when(s == 0)
     def _():
-        cr[0] = jnp.zeros((CHUNKS, 64, WIDE), bf16)
+        cr[0] = jnp.zeros((CHUNKS, SLICE, WIDE), bf16)
 
     @pl.when(s == N_SEQ - 1)
     def _():
-        cr[1] = jnp.zeros((CHUNKS, 64, WIDE), bf16)
+        cr[1] = jnp.zeros((CHUNKS, SLICE, WIDE), bf16)
 
     def part_tile(i, _):
         m = lax.div(i, 4)
@@ -335,15 +350,8 @@
         group = lax.rem(i, 2)
 
         for n, steps in (
-            (1, ((2, 0),)), (4, ((2, 1),)), (6, ((3, 0),)),
-        ):
-            @pl.when(i == n)
-            def _():
-                for j, mm in steps:
-                    ring_step(j, mm)
-
-        for n, steps in (
-            (3, ((1, 0),)), (5, ((1, 1),)), (7, ((1, 2), (2, 0))),
+            (3, ((1, 0),)), (4, ((1, 1),)), (5, ((1, 2),)), (6, ((1, 3),)),
+            (7, ((1, 4), (2, 0))),
         ):
             @pl.when(i == n)
             def _():
@@ -357,11 +365,16 @@
         return 0
 
     lax.fori_loop(0, 8, part_tile, 0)
-    ring_step(3, 1)
-
+    chain(1, 5)
+    chain(2, 1)
+
+    for a in range(2):
+        for i in (0, 2):
+            near_wait(a, i)
+        for i in range(4):
+            far_wait(a, i)
     ld_q.wait()
     ld_r.wait()
-    ring_wait(3, 0)
     r = rv[...]
     r_hi = r.astype(bf16)
     r_lo = (r - r_hi.astype(f32)).astype(bf16)
@@ -390,71 +403,82 @@
                 total = total + jnp.where(go[k][d] == o, 1.0, 0.0) * fv[d, (k + TOUCH - 1) % TOUCH]
         return total
 
-    def normalized(i, _):
-        early = i < 2 * (TOUCH - 1)
-        m = jnp.where(early, lax.div(i, TOUCH - 1), i - 2 * (TOUCH - 1))
-        k = jnp.where(early, lax.rem(i, TOUCH - 1) + 1, 0)
-        row = jnp.where(early, k - 1, TOUCH - 1) * 64 + m * 32
+    def moments_of(m, z, cc):
+        a = mom[z, 0, m, :, cc].astype(f32)
+        b = mom[z, 1, m, :, cc].astype(f32)
+        return (
+            BETA_ONE * jnp.concatenate([a[:8], b[:8]], axis=0),
+            BETA_TWO * jnp.concatenate([a[8:], b[8:]], axis=0),
+        )
+
+    def normalize(scaled, g):
+        first = scaled[0] + (1.0 - BETA_ONE) * g
+        second = scaled[1] + (1.0 - BETA_TWO) * (g * g)
+        root = second * lax.rsqrt(second) + EPSILON
+        return (first * lax.rsqrt(root * root)).astype(bf16)
+
+    def rank_side(k, m, side, n):
+        row = (k + TOUCH - 1) % TOUCH * 64 + m * 32
+        u = jnp.dot(r2, n, preferred_element_type=f32)
+        u = u[:KR] + u[KR:]
+        hi = u.astype(bf16)
+        uv[side, pl.ds(pl.multiple_of(row, 32), 16), :] = hi
+        uv[side, pl.ds(pl.multiple_of(row + 16, 16), 16), :] = (u - hi.astype(f32)).astype(bf16)
+
+    def scale_moments(m, side):
+        cc = half_rows(side)
+        for z in range(N_Z):
+            for i, v in enumerate(moments_of(m, z, cc)):
+                scaled[i, z * 16:z * 16 + 16, :] = v
+
+    def seven(i, _):
+        m = lax.rem(i, 2)
+        side = lax.div(i, 2)
         for n, steps in (
-            (0, ((1, 3), (2, 1))), (3, ((2, 2),)), (6, ((2, 3),)),
+            (0, ((1, 6), (2, 2))), (1, ((1, 7), (2, 3))), (2, ((2, 4),)), (3, ((2, 5),)),
         ):
             @pl.when(i == n)
             def _():
                 for place, c in steps:
                     chain(place, c)
 
-        @pl.when(i == TOUCH - 1)
-        def _():
-            ring_wait(3, 1)
-
-        @pl.when(i == 2 * (TOUCH - 1))
-        def _():
-            for d in range(SIDES):
-                widths(d, 0, TOUCH - 1)
-
-            def place_most(o, _):
-                facc[o] = placed(o, jnp.zeros((2 * KR, KD), f32), range(1, TOUCH))
-                return 0
-
-            lax.fori_loop(0, GROUP, place_most, 0)
-            for d in range(SIDES):
-                @pl.when(places[d] == N_SEQ - 1)
-                def _():
-                    for c in range(CHUNKS):
-                        chain_copy(d, c).wait_recv()
-
-            for d in range(SIDES):
-                cc = slice(d * WIDE, (d + 1) * WIDE)
-                for c in range(CHUNKS):
-                    rr = slice((c % 2) * 64, (c % 2) * 64 + 64)
-                    parts[1 - c // 2, rr, cc] = (
-                        parts[1 - c // 2, rr, cc].astype(f32)
-                        + begins[d] * cr[d, c].astype(f32)).astype(bf16)
-
-        for c in range(COLS // TILE):
-            cc = slice(c * TILE, (c + 1) * TILE)
-            rows = []
-            for z in range(N_Z):
-                a = mom[m, z, 0, :, cc].astype(f32)
-                b = mom[m, z, 1, :, cc].astype(f32)
-                m1 = jnp.concatenate([a[:8], b[:8]], axis=0)
-                m2 = jnp.concatenate([a[8:], b[8:]], axis=0)
-                g = parts[m, pl.ds(pl.multiple_of(k * RANK + z * 16, 16), 16), cc].astype(f32)
-                first = BETA_ONE * m1 + (1.0 - BETA_ONE) * g
-                second = BETA_TWO * m2 + (1.0 - BETA_TWO) * (g * g)
-                root = second * lax.rsqrt(second) + EPSILON
-                rows.append((first * lax.rsqrt(root * root)).astype(bf16))
-            u = jnp.dot(r2, jnp.concatenate(rows, axis=0), preferred_element_type=f32)
-            u = u[:KR] + u[KR:]
-            hi = u.astype(bf16)
-            side = c // 2
-            uc = slice((c % 2) * TILE, (c % 2) * TILE + TILE)
-            uv[side, pl.ds(pl.multiple_of(row, 32), 16), uc] = hi
-            uv[side, pl.ds(pl.multiple_of(row + 16, 16), 16), uc] = (
-                u - hi.astype(f32)).astype(bf16)
-        return 0
-
-    lax.fori_loop(0, 2 * TOUCH, normalized, 0)
+        scale_moments(m, side)
+        for k in range(1, TOUCH):
+            g = parts[m, k * RANK:(k + 1) * RANK, half_rows(side)].astype(f32)
+            rank_side(k, m, side, normalize((scaled[0], scaled[1]), g))
+        return 0
+
+    lax.fori_loop(0, 4, seven, 0)
+    chain(2, 6)
+    chain(2, 7)
+
+    for d in range(SIDES):
+        widths(d, 0, TOUCH - 1)
+
+    def place_most(o, _):
+        facc[o] = placed(o, jnp.zeros((2 * KR, KD), f32), range(1, TOUCH))
+        return 0
+
+    lax.fori_loop(0, GROUP, place_most, 0)
+
+    for d in range(SIDES):
+        @pl.when(places[d] == N_SEQ - 1)
+        def _():
+            for c in range(CHUNKS):
+                chain_copy(d, c).wait_recv()
+
+    def slot_zero(i, _):
+        m = lax.rem(i, 2)
+        side = lax.div(i, 2)
+        scale_moments(m, side)
+        begin = jnp.where(side == 0, begins[0], begins[1])
+        came = jnp.concatenate(
+            [cr[side, (1 - m) * (CHUNKS // 2) + c].astype(f32) for c in range(CHUNKS // 2)], axis=0)
+        g = parts[m, :RANK, half_rows(side)].astype(f32) + begin * came
+        rank_side(0, m, side, normalize((scaled[0], scaled[1]), g))
+        return 0
+
+    lax.fori_loop(0, 4, slot_zero, 0)
 
     for d in range(SIDES):
         widths(d, TOUCH - 1, 1)
@@ -475,7 +499,8 @@
         return 0
 
     lax.fori_loop(0, GROUP, place, 0)
-    frecv[me] = fsend[me]
+    own_feature = pltpu.make_async_copy(fsend.at[me], frecv.at[me], f_ss.at[me])
+    own_feature.start()
 
     lax.fori_loop(3, 4, main_tile, 0)
 
@@ -502,21 +527,15 @@
 
     lax.fori_loop(1, GROUP, arrive, 0)
 
-    def add(o, total):
-        return total + frecv[o].astype(f32)
-
-    feat = lax.fori_loop(0, GROUP, add, jnp.zeros((2 * KR, KD), f32))
-    feat_ref[pl.ds(0, 2 * KR, stride=2), :] = feat[:, :128]
-    feat_ref[pl.ds(1, 2 * KR, stride=2), :] = feat[:, 128:]
-
     for m in range(2):
         ex1(m).wait_send()
         ex2(m).wait_send()
         ex3(m, core).wait_send()
-        mx(m, xh).wait_send()
-        for j in range(4):
-            for c in ring(j, m, 0):
-                c.wait_send()
+    mx(xh).wait_send()
+    for a in range(2):
+        for i in range(4):
+            near_copy(a, i).wait_send()
+            far_copy(a, i).wait_send()
 
     for d in range(SIDES):
         @pl.when(places[d] < N_SEQ - 1)
@@ -529,23 +548,55 @@
         return 0
 
     lax.fori_loop(1, GROUP, left, 0)
+    own_feature.wait()
     for i in range(BLK // TILE):
         out_copy(i).wait()
 
 
+def finish(att_in, feat_in, att_out, feat_out, buf, fbuf, fsum, in_sem, out_sem, f_in, f_out):
+    def piece(i):
+        return pl.ds(i * (BLK // PIECES), BLK // PIECES)
+
+    def load(i):
+        return pltpu.make_async_copy(att_in.at[piece(i), :], buf.at[piece(i), :], in_sem.at[i])
+
+    def store(i):
+        return pltpu.make_async_copy(buf.at[piece(i), :], att_out.at[piece(i), :], out_sem.at[i])
+
+    features = pltpu.make_async_copy(feat_in, fbuf, f_in)
+    features.start()
+    for i in range(PIECES):
+        load(i).start()
+    for i in range(PIECES):
+        load(i).wait()
+        store(i).start()
+    features.wait()
+
+    def add(o, total):
+        return total + fbuf[o].astype(f32)
+
+    feat = lax.fori_loop(0, GROUP, add, jnp.zeros((2 * KR, KD), f32))
+    fsum[pl.ds(0, 2 * KR, stride=2), :] = feat[:, :128]
+    fsum[pl.ds(1, 2 * KR, stride=2), :] = feat[:, 128:]
+    result = pltpu.make_async_copy(fsum, feat_out, f_out)
+    result.start()
+    result.wait()
+    for i in range(PIECES):
+        store(i).wait()
+
+
 def per_device(x, g, a, b, w, m1, m2, r, q, bounds, owner):
     any_ = pl.BlockSpec(memory_space=pl.ANY)
-    vmem = pl.BlockSpec(memory_space=pltpu.VMEM)
     dma = pltpu.SemaphoreType.DMA
     V = pltpu.VMEM
-    att, feat = pl.pallas_call(
+    att, arrived = pl.pallas_call(
         kernel,
         out_shape=(
             jax.ShapeDtypeStruct((BLK, COLS), bf16),
-            jax.ShapeDtypeStruct((4 * KR, KD // 2), f32),
+            jax.ShapeDtypeStruct((GROUP, 2 * KR, KD), bf16),
         ),
         in_specs=[any_] * 11,
-        out_specs=(any_, vmem),
+        out_specs=(any_, any_),
         scratch_shapes=[
             V((2, BLK, COLS), bf16), V((BLK, WIDTH), bf16), V((COLS, WIDTH), bf16),
             V((2, COLS, RANK), bf16), V((RANK, COLS), bf16), V((COLS, KD), bf16),
@@ -556,13 +607,13 @@
             V((2, HALF, RANK), bf16), V((2, HALF, RANK), bf16),
             V((2, 2, HALF, RANK), bf16), V((2 * RANK, BLK), bf16),
             V((2, TOUCH * RANK, COLS), bf16),
-            V((SIDES, CHUNKS, 64, WIDE), bf16), V((SIDES, CHUNKS, 64, WIDE), bf16),
-            V((2, N_Z, 2, 16, COLS), bf16),
+            V((SIDES, CHUNKS, SLICE, WIDE), bf16), V((SIDES, CHUNKS, SLICE, WIDE), bf16),
+            V((N_Z, 2, 2, 16, COLS), bf16), V((2, RANK, WIDE), f32),
             V((SIDES, TOUCH * 64, WIDE), bf16), V((SIDES, TOUCH, 2 * KR, KD), f32),
             V((GROUP, 2 * KR, KD), f32),
-            V((GROUP, 2 * KR, KD), bf16), V((GROUP, 2 * KR, KD), bf16),
-            dma((22,)), dma((4,)), dma((3, 2)), dma((3, 2)), dma((2,)), dma((2,)),
-            dma((4, 2, 2)), dma((4, 2, 2)), dma((SIDES, CHUNKS)), dma((SIDES, CHUNKS)),
+            V((GROUP, 2 * KR, KD), bf16),
+            dma((24,)), dma((4,)), dma((3, 2)), dma((3, 2)), dma(()), dma(()),
+            dma((2, 4)), dma((2, 4)), dma((2, 4)), dma((2, 4)), dma((SIDES, CHUNKS)), dma((SIDES, CHUNKS)),
             dma((GROUP,)), dma((GROUP,)),
         ],
         compiler_params=pltpu.CompilerParams(
@@ -572,6 +623,21 @@
         x.reshape(BLK, COLS), g.reshape(BLK, WIDTH), a, b, w, m1, m2, r, q,
         bounds.reshape(2, EX), owner.reshape(1, EX),
     )
+    att, feat = pl.pallas_call(
+        finish,
+        out_shape=(
+            jax.ShapeDtypeStruct((BLK, COLS), bf16),
+            jax.ShapeDtypeStruct((4 * KR, KD // 2), f32),
+        ),
+        in_specs=[any_, any_],
+        out_specs=(any_, any_),
+        scratch_shapes=[
+            V((BLK, COLS), bf16), V((GROUP, 2 * KR, KD), bf16), V((4 * KR, KD // 2), f32),
+            dma((PIECES,)), dma((PIECES,)), dma(()), dma(()),
+        ],
+        compiler_params=pltpu.CompilerParams(vmem_limit_bytes=VLIMIT * 2**20),
+        name="finish",
+    )(att, arrived)
     return att.reshape(1, BLK, COLS), feat.reshape(1, 1, 2 * KR * KD)
 
 

time: 52.4 us -> 47 us (0.90)
  local copies, waits for them, and re-layouts: 3.7 us -> 0 us
  Pallas kernels: 47.9 us -> 46.2 us
    pallas_call x1, Pallas kernels: 47.9 us -> 43.8 us  [per_device(): pl.pallas_call(kernel, out_shape=(jax.ShapeDtypeStruct((BLK, COLS), bf16)...]
    unnamed x4 -> x0, local copies, waits for them, and re-layouts: 3.7 us -> none
    pallas_call x0 -> x1, Pallas kernels: none -> 2.45 us  [per_device(): pl.pallas_call(finish, out_shape=(jax.ShapeDtypeStruct((BLK, COLS), bf16)...]
where the time goes in v4:
time: 47 us; the launch traced here: 46.9 us
  Pallas kernels  46.2 us (98%)
  between operations  0.64 us (1%)
    pallas_call x1, Pallas kernels, per_device(): pl.pallas_call(kernel, out_shape=(jax.ShapeDtypeStruct((BLK, COLS), bf16)...  43.8 us
    pallas_call x1, Pallas kernels, per_device(): pl.pallas_call(finish, out_shape=(jax.ShapeDtypeStruct((BLK, COLS), bf16)...  2.45 us

profile of v4, /device:TPU:1, one launch (start us, length us, event | category | flops | bytes accessed | tf_op | source)
XLA Modules:
  0.0 46.9 jit_solution(14927128172981099982)
XLA Ops:
  0.6 43.8 %step.1 = (bf16[1024,1024]{1,0:T(8,128)(2,1)}, bf16[16,32,256]{2,1,0:T(8,128)(2,1)}) custom-call(bf16[1024,1024]{1,0:T(8,128)(2,1)} %bitcast.6, bf16[1024,4096]{1,0:T(8,128)(2,1)} %bitcast.5, bf16[1024,128]{1,0:T(8,128)(2,1)} %a_hbm.1, bf16[128,1024]{1,0:T(8,128)(2,1)} %b_hbm.1, bf16[1024,4096]{1,0:T(8,128)(2,1)} %w_hbm.1, f32[2,8,1024]{2,1,0:T(8,128)} %m1_hbm.1, ...), custom_call_target="tpu_custom_call" | custom-call | tf_op jit(solution)/shard_map/step/pallas_call | solution.py:592
  44.4 2.5 %finish.1 = (bf16[1024,1024]{1,0:T(8,128)(2,1)}, f32[64,128]{1,0:T(8,128)}) custom-call(bf16[1024,1024]{1,0:T(8,128)(2,1)} %get-tuple-element.6.att_in, bf16[16,32,256]{2,1,0:T(8,128)(2,1)} %get-tuple-element.7.feat_in), custom_call_target="tpu_custom_call" | custom-call | tf_op jit(solution)/shard_map/finish/pallas_call | solution.py:626

commit v5 on v4

--- a/solution.py
+++ b/solution.py
@@ -83,8 +83,8 @@
     own_g = [load(8 + 4 * h, xg.at[1, half_rows(h), :], gv.at[half_rows(h), col(0)])
              for h in range(2)]
     ld_w = [
-        load(16 + i, w_hbm.at[pl.ds(i * WIDE, WIDE), :], wv.at[pl.ds(i * WIDE, WIDE), :])
-        for i in range(2)
+        load(16 + i, w_hbm.at[pl.ds(i * TILE, TILE), :], wv.at[pl.ds(i * TILE, TILE), :])
+        for i in range(4)
     ]
     ld_q = load(20, q_hbm.at[col(0), :], qv)
     ld_r = load(21, r_hbm, rv)
@@ -176,6 +176,12 @@
         for i in range(4):
             far_copy(a, i).start()
 
+    ld_b.wait()
+    ab[0] = bv[...].T
+    ld_m1.wait()
+    ld_m2.wait()
+    for mm in range(2):
+        mom[zi, xh, mm] = jnp.concatenate([m1v[mm], m2v[mm]], axis=0).astype(bf16)
     ld_a.wait()
 
     def partial(i, _):
@@ -183,11 +189,6 @@
         late = lax.rem(i, 2)
         rows = half_rows(jnp.where(late == 1, core, 1 - core))
 
-        @pl.when(i == 2)
-        def _():
-            ld_b.wait()
-            ab[0] = bv[...].T
-
         for n in range(4):
             @pl.when(i == n)
             def _():
@@ -203,14 +204,10 @@
         def _():
             lowh[m] = p
 
-        @pl.when(i == 0)
+        @pl.when(i == 1)
         def _():
             pl.semaphore_wait(barrier, GROUP - 1 + 5)
             ex1(1).start()
-            ld_m1.wait()
-            ld_m2.wait()
-            for mm in range(2):
-                mom[zi, xh, mm] = jnp.concatenate([m1v[mm], m2v[mm]], axis=0).astype(bf16)
             mx(xh).start()
             round_one(0)
 
@@ -230,33 +227,6 @@
     own_g[0].wait()
     ld_w[0].wait()
     second(0)
-
-    def main_tile(i, _):
-        @pl.when(i == 1)
-        def _():
-            for c in ld_g[1]:
-                c.wait()
-            own_g[1].wait()
-
-        @pl.when(i == 1)
-        def _():
-            round_one(1)
-
-        @pl.when(i == 2)
-        def _():
-            ld_w[1].wait()
-            third(1)
-            round_two(0)
-
-        rows = half_rows(lax.rem(i, 2))
-        cc = pl.ds(pl.multiple_of(lax.div(i, 2) * WIDE, WIDE), WIDE)
-        acc[rows, cc] = lax.dot_general(
-            gv[rows, :], wv[cc, :], NT, preferred_element_type=f32)
-        return 0
-
-    lax.fori_loop(0, 3, main_tile, 0)
-
-    third(0)
 
     ld_bounds.wait()
     ld_owner.wait()
@@ -307,34 +277,58 @@
                         cs[d, c].astype(f32) + keeps[d] * cr[d, c].astype(f32)).astype(bf16)
                 chain_copy(d, c).start()
 
-    def far(i, _):
-        m = 1 - lax.div(i, 2)
-        side = lax.rem(i, 2)
-
-        for mm in (1, 0):
-            @pl.when(i == 2 * (1 - mm))
+    def far(m):
+        ex3(m, 1 - core).wait_recv()
+        for h in range(2):
+            low_t[m * RANK:(m + 1) * RANK, h * HALF:(h + 1) * HALF] = (
+                low[h, m].astype(f32) * SCALE).T.astype(bf16)
+
+        def one(side, _):
+            left = low_t[m * RANK:(m + 1) * RANK, :] * mask_of(side, n_slots)
+            p = jnp.dot(left, xg[m, :, half_rows(side)], preferred_element_type=f32).astype(bf16)
+            for c in range(CHUNKS // 2):
+                cs[side, (1 - m) * (CHUNKS // 2) + c] = p[c * SLICE:(c + 1) * SLICE]
+            return 0
+
+        lax.fori_loop(0, SIDES, one, 0)
+        for c in range(CHUNKS // 2):
+            chain(0, (1 - m) * (CHUNKS // 2) + c)
+
+    def main_tile(i, _):
+        @pl.when(i == 1)
+        def _():
+            for c in ld_g[1]:
+                c.wait()
+            own_g[1].wait()
+
+        for n in (1, 2, 3):
+            @pl.when(i == 2 * n)
             def _():
-                if mm == 0:
-                    for c in range(CHUNKS // 2):
-                        chain(0, c)
-                ex3(mm, 1 - core).wait_recv()
-
-        @pl.when(side == 0)
-        def _():
-            for h in range(2):
-                low_t[rank_rows(m), h * HALF:(h + 1) * HALF] = (
-                    low[h, m].astype(f32) * SCALE).T.astype(bf16)
-
-        left = low_t[rank_rows(m), :] * mask_of(side, n_slots)
-        p = jnp.dot(left, xg[m, :, half_rows(side)], preferred_element_type=f32).astype(bf16)
-        for c in range(CHUNKS // 2):
-            cs[side, (1 - m) * (CHUNKS // 2) + c] = p[c * SLICE:(c + 1) * SLICE]
-        return 0
-
-    lax.fori_loop(0, 4, far, 0)
-    for c in range(CHUNKS // 2, CHUNKS):
-        chain(0, c)
-    round_two(1)
+                ld_w[n].wait()
+
+        @pl.when(i == 3)
+        def _():
+            round_one(1)
+
+        @pl.when(i == 4)
+        def _():
+            third(1)
+
+        @pl.when(i == 5)
+        def _():
+            far(1)
+            third(0)
+            round_two(0)
+
+        rows = half_rows(lax.rem(i, 2))
+        cc = pl.ds(pl.multiple_of(lax.div(i, 2) * TILE, TILE), TILE)
+        acc[rows, cc] = lax.dot_general(
+            gv[rows, :], wv[cc, :], NT, preferred_element_type=f32)
+        return 0
+
+    lax.fori_loop(0, 6, main_tile, 0)
+
+    far(0)
 
     @pl.when(s == 0)
     def _():
@@ -350,14 +344,18 @@
         group = lax.rem(i, 2)
 
         for n, steps in (
-            (3, ((1, 0),)), (4, ((1, 1),)), (5, ((1, 2),)), (6, ((1, 3),)),
-            (7, ((1, 4), (2, 0))),
+            (1, ((1, 0),)), (2, ((1, 1),)), (3, ((1, 2),)), (4, ((1, 3),)),
+            (5, ((1, 4), (2, 0))), (6, ((1, 5), (2, 1))), (7, ((1, 6), (2, 2))),
         ):
             @pl.when(i == n)
             def _():
                 for place, c in steps:
                     chain(place, c)
 
+        @pl.when(i == 2)
+        def _():
+            round_two(1)
+
         low_m = low_t[rank_rows(m), :]
         left = jnp.concatenate([low_m * mask_of(side, group * 4 + k) for k in range(4)], axis=0)
         p = jnp.dot(left, xg[m, :, half_rows(side)], preferred_element_type=f32)
@@ -365,8 +363,8 @@
         return 0
 
     lax.fori_loop(0, 8, part_tile, 0)
-    chain(1, 5)
-    chain(2, 1)
+    chain(1, 7)
+    chain(2, 3)
 
     for a in range(2):
         for i in (0, 2):
@@ -422,20 +420,22 @@
         u = jnp.dot(r2, n, preferred_element_type=f32)
         u = u[:KR] + u[KR:]
         hi = u.astype(bf16)
-        uv[side, pl.ds(pl.multiple_of(row, 32), 16), :] = hi
-        uv[side, pl.ds(pl.multiple_of(row + 16, 16), 16), :] = (u - hi.astype(f32)).astype(bf16)
+        if not isinstance(row, int):
+            row = pl.multiple_of(row, 32)
+        uv[side, pl.ds(row, 16), :] = hi
+        uv[side, pl.ds(row + 16, 16), :] = (u - hi.astype(f32)).astype(bf16)
 
     def scale_moments(m, side):
         cc = half_rows(side)
         for z in range(N_Z):
             for i, v in enumerate(moments_of(m, z, cc)):
-                scaled[i, z * 16:z * 16 + 16, :] = v
+                scaled[2 * side + m, i, z * 16:z * 16 + 16, :] = v
 
     def seven(i, _):
         m = lax.rem(i, 2)
         side = lax.div(i, 2)
         for n, steps in (
-            (0, ((1, 6), (2, 2))), (1, ((1, 7), (2, 3))), (2, ((2, 4),)), (3, ((2, 5),)),
+            (0, ((2, 4),)), (1, ((2, 5),)), (2, ((2, 6), (2, 7))),
         ):
             @pl.when(i == n)
             def _():
@@ -445,12 +445,10 @@
         scale_moments(m, side)
         for k in range(1, TOUCH):
             g = parts[m, k * RANK:(k + 1) * RANK, half_rows(side)].astype(f32)
-            rank_side(k, m, side, normalize((scaled[0], scaled[1]), g))
+            rank_side(k, m, side, normalize((scaled[i, 0], scaled[i, 1]), g))
         return 0
 
     lax.fori_loop(0, 4, seven, 0)
-    chain(2, 6)
-    chain(2, 7)
 
     for d in range(SIDES):
         widths(d, 0, TOUCH - 1)
@@ -467,18 +465,13 @@
             for c in range(CHUNKS):
                 chain_copy(d, c).wait_recv()
 
-    def slot_zero(i, _):
-        m = lax.rem(i, 2)
-        side = lax.div(i, 2)
-        scale_moments(m, side)
-        begin = jnp.where(side == 0, begins[0], begins[1])
+    for i in range(4):
+        m = i % 2
+        side = i // 2
         came = jnp.concatenate(
             [cr[side, (1 - m) * (CHUNKS // 2) + c].astype(f32) for c in range(CHUNKS // 2)], axis=0)
-        g = parts[m, :RANK, half_rows(side)].astype(f32) + begin * came
-        rank_side(0, m, side, normalize((scaled[0], scaled[1]), g))
-        return 0
-
-    lax.fori_loop(0, 4, slot_zero, 0)
+        g = parts[m, :RANK, side * WIDE:(side + 1) * WIDE].astype(f32) + begins[side] * came
+        rank_side(0, m, side, normalize((scaled[i, 0], scaled[i, 1]), g))
 
     for d in range(SIDES):
         widths(d, TOUCH - 1, 1)
@@ -502,7 +495,7 @@
     own_feature = pltpu.make_async_copy(fsend.at[me], frecv.at[me], f_ss.at[me])
     own_feature.start()
 
-    lax.fori_loop(3, 4, main_tile, 0)
+    lax.fori_loop(6, 8, main_tile, 0)
 
     def out_copy(i):
         rows = pl.ds(pl.multiple_of(i * TILE, TILE), TILE)
@@ -608,7 +601,7 @@
             V((2, 2, HALF, RANK), bf16), V((2 * RANK, BLK), bf16),
             V((2, TOUCH * RANK, COLS), bf16),
             V((SIDES, CHUNKS, SLICE, WIDE), bf16), V((SIDES, CHUNKS, SLICE, WIDE), bf16),
-            V((N_Z, 2, 2, 16, COLS), bf16), V((2, RANK, WIDE), f32),
+            V((N_Z, 2, 2, 16, COLS), bf16), V((4, 2, RANK, WIDE), f32),
             V((SIDES, TOUCH * 64, WIDE), bf16), V((SIDES, TOUCH, 2 * KR, KD), f32),
             V((GROUP, 2 * KR, KD), f32),
             V((GROUP, 2 * KR, KD), bf16),

time: 47 us -> 44.4 us (0.945)
  Pallas kernels: 46.2 us -> 43.6 us
    pallas_call x1, Pallas kernels: 43.8 us -> 41.2 us  [per_device(): pl.pallas_call(kernel, out_shape=(jax.ShapeDtypeStruct((BLK, COLS), bf16)...]
where the time goes in v5:
time: 44.4 us; the launch traced here: 44.3 us
  Pallas kernels  43.6 us (98%)
  between operations  0.64 us (1%)
    pallas_call x1, Pallas kernels, per_device(): pl.pallas_call(kernel, out_shape=(jax.ShapeDtypeStruct((BLK, COLS), bf16)...  41.2 us
    pallas_call x1, Pallas kernels, per_device(): pl.pallas_call(finish, out_shape=(jax.ShapeDtypeStruct((BLK, COLS), bf16)...  2.45 us

profile of v5, /device:TPU:1, one launch (start us, length us, event | category | flops | bytes accessed | tf_op | source)
XLA Modules:
  0.0 44.3 jit_solution(7854677648123944413)
XLA Ops:
  0.6 41.2 %step.1 = (bf16[1024,1024]{1,0:T(8,128)(2,1)}, bf16[16,32,256]{2,1,0:T(8,128)(2,1)}) custom-call(bf16[1024,1024]{1,0:T(8,128)(2,1)} %bitcast.6, bf16[1024,4096]{1,0:T(8,128)(2,1)} %bitcast.5, bf16[1024,128]{1,0:T(8,128)(2,1)} %a_hbm.1, bf16[128,1024]{1,0:T(8,128)(2,1)} %b_hbm.1, bf16[1024,4096]{1,0:T(8,128)(2,1)} %w_hbm.1, f32[2,8,1024]{2,1,0:T(8,128)} %m1_hbm.1, ...), custom_call_target="tpu_custom_call" | custom-call | tf_op jit(solution)/shard_map/step/pallas_call | solution.py:585
  41.8 2.5 %finish.1 = (bf16[1024,1024]{1,0:T(8,128)(2,1)}, f32[64,128]{1,0:T(8,128)}) custom-call(bf16[1024,1024]{1,0:T(8,128)(2,1)} %get-tuple-element.6.att_in, bf16[16,32,256]{2,1,0:T(8,128)(2,1)} %get-tuple-element.7.feat_in), custom_call_target="tpu_custom_call" | custom-call | tf_op jit(solution)/shard_map/finish/pallas_call | solution.py:619

commit v6 on v5

--- a/solution.py
+++ b/solution.py
@@ -10,6 +10,7 @@
 BETA_ONE = 0.9
 BETA_TWO = 0.999
 EPSILON = 1e-08
+SQUARE = (1.0 - BETA_TWO) / (1.0 - BETA_ONE) ** 2
 
 N_DP, N_SEQ, N_TP = 16, 4, 4
 GROUP = N_SEQ * N_TP
@@ -167,7 +168,7 @@
     def round_one(a):
         if a == 1:
             mx(1 - xh).wait_recv()
-        for i in range(4):
+        for i in (1, 3, 0, 2):
             near_copy(a, i).start()
 
     def round_two(a):
@@ -306,7 +307,7 @@
             def _():
                 ld_w[n].wait()
 
-        @pl.when(i == 3)
+        @pl.when(i == 2)
         def _():
             round_one(1)
 
@@ -352,14 +353,14 @@
                 for place, c in steps:
                     chain(place, c)
 
-        @pl.when(i == 2)
+        @pl.when(i == 0)
         def _():
             round_two(1)
 
         low_m = low_t[rank_rows(m), :]
         left = jnp.concatenate([low_m * mask_of(side, group * 4 + k) for k in range(4)], axis=0)
         p = jnp.dot(left, xg[m, :, half_rows(side)], preferred_element_type=f32)
-        parts[m, half_rows(group), half_rows(side)] = p.astype(bf16)
+        parts[m, half_rows(group), half_rows(side)] = (p * (1.0 - BETA_ONE)).astype(bf16)
         return 0
 
     lax.fori_loop(0, 8, part_tile, 0)
@@ -410,8 +411,8 @@
         )
 
     def normalize(scaled, g):
-        first = scaled[0] + (1.0 - BETA_ONE) * g
-        second = scaled[1] + (1.0 - BETA_TWO) * (g * g)
+        first = scaled[0] + g
+        second = scaled[1] + SQUARE * (g * g)
         root = second * lax.rsqrt(second) + EPSILON
         return (first * lax.rsqrt(root * root)).astype(bf16)
 
@@ -470,7 +471,7 @@
         side = i // 2
         came = jnp.concatenate(
             [cr[side, (1 - m) * (CHUNKS // 2) + c].astype(f32) for c in range(CHUNKS // 2)], axis=0)
-        g = parts[m, :RANK, side * WIDE:(side + 1) * WIDE].astype(f32) + begins[side] * came
+        g = parts[m, :RANK, side * WIDE:(side + 1) * WIDE].astype(f32) + begins[side] * (1.0 - BETA_ONE) * came
         rank_side(0, m, side, normalize((scaled[i, 0], scaled[i, 1]), g))
 
     for d in range(SIDES):

time: 44.4 us -> 44.4 us (level)
  no operation moved by 1% of the time
where the time goes in v6:
time: 44.4 us; the launch traced here: 44.3 us
  Pallas kernels  43.6 us (98%)
  between operations  0.64 us (1%)
    pallas_call x1, Pallas kernels, per_device(): pl.pallas_call(kernel, out_shape=(jax.ShapeDtypeStruct((BLK, COLS), bf16)...  41.2 us
    pallas_call x1, Pallas kernels, per_device(): pl.pallas_call(finish, out_shape=(jax.ShapeDtypeStruct((BLK, COLS), bf16)...  2.45 us

profile of v6, /device:TPU:1, one launch (start us, length us, event | category | flops | bytes accessed | tf_op | source)
XLA Modules:
  0.0 44.3 jit_solution(17127329006210288823)
XLA Ops:
  0.6 41.2 %step.1 = (bf16[1024,1024]{1,0:T(8,128)(2,1)}, bf16[16,32,256]{2,1,0:T(8,128)(2,1)}) custom-call(bf16[1024,1024]{1,0:T(8,128)(2,1)} %bitcast.6, bf16[1024,4096]{1,0:T(8,128)(2,1)} %bitcast.5, bf16[1024,128]{1,0:T(8,128)(2,1)} %a_hbm.1, bf16[128,1024]{1,0:T(8,128)(2,1)} %b_hbm.1, bf16[1024,4096]{1,0:T(8,128)(2,1)} %w_hbm.1, f32[2,8,1024]{2,1,0:T(8,128)} %m1_hbm.1, ...), custom_call_target="tpu_custom_call" | custom-call | tf_op jit(solution)/shard_map/step/pallas_call | solution.py:586
  41.8 2.5 %finish.1 = (bf16[1024,1024]{1,0:T(8,128)(2,1)}, f32[64,128]{1,0:T(8,128)}) custom-call(bf16[1024,1024]{1,0:T(8,128)(2,1)} %get-tuple-element.6.att_in, bf16[16,32,256]{2,1,0:T(8,128)(2,1)} %get-tuple-element.7.feat_in), custom_call_target="tpu_custom_call" | custom-call | tf_op jit(solution)/shard_map/finish/pallas_call | solution.py:620

commit v7 on v6

--- a/solution.py
+++ b/solution.py
@@ -389,12 +389,10 @@
         go.append((left_go, jnp.where(done, owner[0, e], -1)))
 
     def widths(side, lo, n):
-        u = uv[side, lo * 64:(lo + n) * 64, :]
+        u = uv[side, lo * 32:(lo + n) * 32, :]
         f = jnp.dot(u, qv[side * WIDE:(side + 1) * WIDE, :], preferred_element_type=f32)
         for i in range(n):
-            v = f[i * 64:(i + 1) * 64]
-            fv[side, lo + i] = jnp.concatenate(
-                [v[:KR] + v[KR:2 * KR], v[2 * KR:3 * KR] + v[3 * KR:]], axis=0)
+            fv[side, lo + i] = f[i * 32:(i + 1) * 32]
 
     def placed(o, total, slots):
         for k in slots:
@@ -417,14 +415,11 @@
         return (first * lax.rsqrt(root * root)).astype(bf16)
 
     def rank_side(k, m, side, n):
-        row = (k + TOUCH - 1) % TOUCH * 64 + m * 32
+        row = (k + TOUCH - 1) % TOUCH * 32 + m * KR
         u = jnp.dot(r2, n, preferred_element_type=f32)
-        u = u[:KR] + u[KR:]
-        hi = u.astype(bf16)
         if not isinstance(row, int):
-            row = pl.multiple_of(row, 32)
-        uv[side, pl.ds(row, 16), :] = hi
-        uv[side, pl.ds(row + 16, 16), :] = (u - hi.astype(f32)).astype(bf16)
+            row = pl.multiple_of(row, KR)
+        uv[side, pl.ds(row, KR), :] = (u[:KR] + u[KR:]).astype(bf16)
 
     def scale_moments(m, side):
         cc = half_rows(side)
@@ -603,7 +598,7 @@
             V((2, TOUCH * RANK, COLS), bf16),
             V((SIDES, CHUNKS, SLICE, WIDE), bf16), V((SIDES, CHUNKS, SLICE, WIDE), bf16),
             V((N_Z, 2, 2, 16, COLS), bf16), V((4, 2, RANK, WIDE), f32),
-            V((SIDES, TOUCH * 64, WIDE), bf16), V((SIDES, TOUCH, 2 * KR, KD), f32),
+            V((SIDES, TOUCH * 32, WIDE), bf16), V((SIDES, TOUCH, 2 * KR, KD), f32),
             V((GROUP, 2 * KR, KD), f32),
             V((GROUP, 2 * KR, KD), bf16),
             dma((24,)), dma((4,)), dma((3, 2)), dma((3, 2)), dma(()), dma(()),

time: 44.4 us -> 44.1 us (level)
  no operation moved by 1% of the time
where the time goes in v7:
time: 44.1 us; the launch traced here: 44 us
  Pallas kernels  43.4 us (98%)
  between operations  0.64 us (1%)
    pallas_call x1, Pallas kernels, per_device(): pl.pallas_call(kernel, out_shape=(jax.ShapeDtypeStruct((BLK, COLS), bf16)...  40.9 us
    pallas_call x1, Pallas kernels, per_device(): pl.pallas_call(finish, out_shape=(jax.ShapeDtypeStruct((BLK, COLS), bf16)...  2.45 us

profile of v7, /device:TPU:1, one launch (start us, length us, event | category | flops | bytes accessed | tf_op | source)
XLA Modules:
  0.0 44.0 jit_solution(13149660158067077821)
XLA Ops:
  0.6 40.9 %step.1 = (bf16[1024,1024]{1,0:T(8,128)(2,1)}, bf16[16,32,256]{2,1,0:T(8,128)(2,1)}) custom-call(bf16[1024,1024]{1,0:T(8,128)(2,1)} %bitcast.6, bf16[1024,4096]{1,0:T(8,128)(2,1)} %bitcast.5, bf16[1024,128]{1,0:T(8,128)(2,1)} %a_hbm.1, bf16[128,1024]{1,0:T(8,128)(2,1)} %b_hbm.1, bf16[1024,4096]{1,0:T(8,128)(2,1)} %w_hbm.1, f32[2,8,1024]{2,1,0:T(8,128)} %m1_hbm.1, ...), custom_call_target="tpu_custom_call" | custom-call | tf_op jit(solution)/shard_map/step/pallas_call | solution.py:581
  41.6 2.5 %finish.1 = (bf16[1024,1024]{1,0:T(8,128)(2,1)}, f32[64,128]{1,0:T(8,128)}) custom-call(bf16[1024,1024]{1,0:T(8,128)(2,1)} %get-tuple-element.6.att_in, bf16[16,32,256]{2,1,0:T(8,128)(2,1)} %get-tuple-element.7.feat_in), custom_call_target="tpu_custom_call" | custom-call | tf_op jit(solution)/shard_map/finish/pallas_call | solution.py:615
